TPU v7x, 512 devices: a whole 4x4x16 slice. The times are simulated.
512 devices in a mesh: box: 32 (over z, core), dir: 16 (over y, x).
Axes of the slice: x: 4, y: 4, z: 16, core: 2. Of those that a mesh axis runs over, the one named last changes fastest.
Arguments:
- fine_density: bfloat16 [4096, 6144], P(('box', 'dir')), may hold values from -6 to 6
- coarse_density: bfloat16 [2048, 12288], P(('box', 'dir')), may hold values from -6 to 6
- fine_operators: bfloat16 [192, 3072], replicated, may hold values from -0.109375 to 0.109375
- coarse_operators: bfloat16 [192, 3072], replicated, may hold values from -0.109375 to 0.109375
- fine_balance: int32 [32], replicated, may hold values from 0 to 31, each once
- coarse_balance: int32 [64], replicated, may hold values from 0 to 63, each once
- fine_sources: int32 [32, 65536], P('dir', 'box'), may hold values from 0 to 4095, as said below
- fine_targets: int32 [32, 65536], P('dir', 'box'), may hold values from 0 to 4095, as said below
- fine_op_ids: int32 [32, 65536], P('dir', 'box'), may hold values from 0 to 15
- coarse_sources: int32 [64, 32768], P('dir', 'box'), may hold values from 0 to 2047, as said below
- coarse_targets: int32 [64, 32768], P('dir', 'box'), may hold values from 0 to 2047, as said below
- coarse_op_ids: int32 [64, 32768], P('dir', 'box'), may hold values from 0 to 15
Outputs:
- fine_local: bfloat16 [4096, 6144], P('box', 'dir')
- coarse_local: bfloat16 [2048, 12288], P('box', 'dir')
Inputs may be any that keep to these rules, and one draw needn't show every extreme that they name: `fine_targets`: pair column p belongs to the Morton range r = p // 2048; its target box lies in boxes r * 128 to (r + 1) * 128 - 1, and the first and last box of every range are named. `fine_sources`: the source of a pair of range r lies in boxes r * 128 - 32 to (r + 1) * 128 + 31, within the grid; in every range the sources at both ends of that span, as far as they lie in the grid, are named. `coarse_targets`: pair column p belongs to the Morton range r = p // 1024; its target box lies in boxes r * 64 to (r + 1) * 64 - 1, and the first and last box of every range are named. `coarse_sources`: the source of a pair of range r lies in boxes r * 64 - 32 to (r + 1) * 64 + 31, within the grid; in every range the sources at both ends of that span, as far as they lie in the grid, are named.
All inputs are finite; a program needn't handle non-finite values.
Results may differ from a plain program's by a relative error of at most 0.001.
Values may be sent and summed in bfloat16 or wider, within the bound.
No kernel may reach another device: no remote copies, remote signals or barrier semaphores. Data moves between devices by JAX's collectives and lax.ppermute only.
A program may use at most 64 MiB of HBM per device.

v0:
```python
import functools

import jax
import jax.numpy as jnp
from jax import lax
from jax.experimental import pallas as pl
from jax.experimental.pallas import tpu as pltpu
from jax.sharding import PartitionSpec as P

RIM = 32
C = 192
NOP = 16
BF = jnp.bfloat16
F32 = jnp.float32


F8 = jnp.float8_e4m3fn
HOT = F8
VMEM = pl.BlockSpec(memory_space=pltpu.VMEM)
SMEM = pl.BlockSpec(memory_space=pltpu.SMEM)
HBM = pl.BlockSpec(memory_space=pltpu.HBM)
ANY = pl.BlockSpec(memory_space=pl.ANY)


def fetch(pairs, sems, first=0):
    copies = [pltpu.make_async_copy(s, d, sems.at[first + i]) for i, (s, d) in enumerate(pairs)]
    for copy in copies:
        copy.start()
    return copies


def pack_kernel(fb, cb, fd, cd, fh, ch, out_ref, fb_s, cb_s, fd_v, cd_v, fh_v, ch_v, fine_wide, coarse_wide, sems):
    copies = fetch(((fb, fb_s), (cb, cb_s), (fd, fd_v), (cd, cd_v), (fh, fh_v), (ch, ch_v)), sems)
    for copy in copies:
        copy.wait()
    fine_wide[0:8, :] = fd_v[...].astype(F32)
    fine_wide[8:16, :] = fh_v[...].astype(F32)
    for k, ref in enumerate((cd_v, ch_v)):
        rows = ref[...].astype(F32)
        coarse_wide[8 * k : 8 * k + 4, :] = rows
        coarse_wide[8 * k + 4 : 8 * k + 8, :] = rows
    low = lax.broadcasted_iota(jnp.int32, (16, 128), 1) < 64
    top = (lax.broadcasted_iota(jnp.int32, (16, 128), 0) & 7) < 4

    def window(ref, wedge):
        odd = lax.rem(wedge, 2)
        start = pl.multiple_of(wedge * C - odd * 64, 128)
        first = ref[:, pl.ds(start, 128)]
        second = ref[:, pl.ds(pl.multiple_of(start + 128, 128), 128)]
        return odd == 1, first, second, pltpu.roll(first, 64, 1), pltpu.roll(second, 64, 1)

    def left(ref, wedge):
        odd, first, second, first_r, second_r = window(ref, wedge)
        head = jnp.where(odd, jnp.where(low, first_r, second_r), first)
        return head, jnp.where(odd, second_r, second)

    def right(ref, wedge):
        odd, first, second, first_r, second_r = window(ref, wedge)
        tail = jnp.where(odd, second, jnp.where(low, first_r, second_r))
        return jnp.where(odd, first, first_r), tail

    def joined(even, odd):
        return even[0], jnp.where(low, even[1], odd[0]), odd[1]

    for peer in range(out_ref.shape[0]):
        parts = joined(left(fine_wide, fb_s[2 * peer]), right(fine_wide, fb_s[2 * peer + 1]))
        upper = joined(left(coarse_wide, cb_s[4 * peer]), right(coarse_wide, cb_s[4 * peer + 1]))
        lower = joined(left(coarse_wide, cb_s[4 * peer + 2]), right(coarse_wide, cb_s[4 * peer + 3]))
        for k in range(3):
            lanes = slice(k * 128, (k + 1) * 128)
            out_ref[peer, 0:16, lanes] = parts[k].astype(BF)
            out_ref[peer, 16:32, lanes] = jnp.where(top, upper[k], lower[k]).astype(BF)


def pack(fine_balance, coarse_balance, fine, coarse, fine_near, coarse_near, peers):
    arrays = (fine, coarse, fine_near, coarse_near)
    return pl.pallas_call(
        pack_kernel,
        out_shape=jax.ShapeDtypeStruct((peers, 32, 2 * C), BF),
        in_specs=[HBM] * 4 + [ANY] * 2,
        out_specs=VMEM,
        scratch_shapes=[pltpu.SMEM(fine_balance.shape, jnp.int32), pltpu.SMEM(coarse_balance.shape, jnp.int32)]
        + [pltpu.VMEM(a.shape, BF) for a in arrays]
        + [
            pltpu.VMEM((16, fine.shape[1]), F32),
            pltpu.VMEM((16, coarse.shape[1]), F32),
            pltpu.SemaphoreType.DMA((6,)),
        ],
        cost_estimate=pl.CostEstimate(flops=4_000_000, bytes_accessed=800_000, transcendentals=0),
        name="pack",
    )(fine_balance, coarse_balance, *arrays)


def op_groups(boxes):
    many = 512 // boxes
    groups = []
    for start in range(0, NOP, 2 * many):
        groups.append([start + 2 * k for k in range(many)])
        groups.append([start + 2 * k + 1 for k in range(many)])
    return groups


def count_slot(slot, column, src_ref, tgt_ref, op_ref, first, n_ref, h_ref, outs, sem, flag_ref, flag_at, tt, st, boxes):
    pairs = src_ref.shape[1]
    target = tgt_ref[pl.ds(slot, 1), :] - first
    source = column(src_ref[pl.ds(slot, 1), :] - first)
    tt[...] = (lax.broadcasted_iota(jnp.int32, (boxes, pairs), 0) == target).astype(F32).astype(BF)
    st[...] = (lax.broadcasted_iota(jnp.int32, (256, pairs), 0) == source).astype(F32).astype(HOT)
    op_rows = jnp.broadcast_to(op_ref[pl.ds(slot, 1), :], (16, pairs))

    def count(ops):
        parts = []
        for o in ops:
            mask = (op_rows == o).astype(F32).astype(BF)
            parts.append((tt[...].reshape(boxes // 16, 16, pairs) * mask[None]).reshape(boxes, pairs).astype(HOT))
        lhs = jnp.concatenate(parts, axis=0)
        return lax.dot_general(lhs, st[...], (((1,), (1,)), ((), ())), preferred_element_type=F32)

    most = jnp.float32(0.0)
    for g, ops in enumerate(op_groups(boxes)):
        found = count(ops)
        n_ref[slot, g * 512 : (g + 1) * 512, :] = found.astype(BF)
        most = jnp.maximum(most, jnp.max(found))
    many = most > 256.0
    flag_ref[flag_at + slot] = many.astype(jnp.int32)

    @pl.when(many)
    def _():
        for g, ops in enumerate(op_groups(boxes)):
            found = count(ops)
            high = jnp.floor(found * (1.0 / 256.0))
            n_ref[slot, g * 512 : (g + 1) * 512, :] = (found - high * 256.0).astype(BF)
            h_ref[g * 512 : (g + 1) * 512, :] = high.astype(BF)
        pltpu.sync_copy(h_ref, outs[1].at[slot])

    pltpu.make_async_copy(n_ref.at[slot], outs[0].at[slot], sem).start()


def fine_column(at):
    halo = jnp.logical_or(at < 0, at >= 128).astype(jnp.int32)
    return ((at & 127) >> 3) * 16 + halo * 8 + (at & 7)


def coarse_column(half):
    def column(at):
        halo = jnp.logical_or(at < 0, at >= 64).astype(jnp.int32)
        return ((at & 63) >> 2) * 16 + halo * 8 + half * 4 + (at & 3)

    return column


def count_kernel(
    firsts, fs, ft, fo, cs, ct, co, fop, cop, fn, fh, cn, ch, flag_ref, fw, cw,
    fs_v, ft_v, fo_v, cs_v, ct_v, co_v, fop_v, cop_v, ftt, fst, ctt, cst,
    fn_v, fh_v, cn_v, ch_v, fw_v, cw_v, sems, out_sems,
):
    copies = fetch(
        ((fs, fs_v), (ft, ft_v), (fo, fo_v), (cs, cs_v), (ct, ct_v), (co, co_v), (fop, fop_v), (cop, cop_v)), sems
    )
    for copy in copies[:6]:
        copy.wait()
    fine_slots, coarse_slots = fs_v.shape[0], cs_v.shape[0]

    def fine(j, _):
        outs, sem = (fn, fh), out_sems.at[j]
        count_slot(j, fine_column, fs_v, ft_v, fo_v, firsts[0], fn_v, fh_v, outs, sem, flag_ref, 0, ftt, fst, 128)
        return 0

    def coarse(j, _):
        outs, sem = (cn, ch), out_sems.at[fine_slots + j]
        column = coarse_column(j >> 1)
        count_slot(
            j, column, cs_v, ct_v, co_v, firsts[1], cn_v, ch_v, outs, sem, flag_ref, fine_slots, ctt, cst, 64
        )
        return 0

    lax.fori_loop(0, fine_slots, fine, 0)
    lax.fori_loop(0, coarse_slots, coarse, 0)
    total = fine_slots + coarse_slots
    done = [pltpu.make_async_copy(fn_v.at[j], fn.at[j], out_sems.at[j]) for j in range(fine_slots)]
    done += [pltpu.make_async_copy(cn_v.at[j], cn.at[j], out_sems.at[fine_slots + j]) for j in range(coarse_slots)]
    for k, (op_ref, w_v, w_ref) in enumerate(((fop_v, fw_v, fw), (cop_v, cw_v, cw))):
        copies[6 + k].wait()
        for o in range(NOP):
            w_v[o * C : (o + 1) * C, :] = op_ref[:, o * C : (o + 1) * C]
        done += fetch(((w_v, w_ref),), out_sems, total + k)
    for copy in done:
        copy.wait()


def counts(firsts, fine_index, coarse_index, fine_operators, coarse_operators, fine_boxes, coarse_boxes):
    fine_slots, fine_pairs = fine_index[0].shape
    coarse_slots, coarse_pairs = coarse_index[0].shape
    fine_shape = (fine_slots, NOP * fine_boxes, 256)
    coarse_shape = (coarse_slots, NOP * coarse_boxes, 256)
    sds = jax.ShapeDtypeStruct
    arrays = (*fine_index, *coarse_index, fine_operators, coarse_operators)
    return pl.pallas_call(
        count_kernel,
        out_shape=(
            sds(fine_shape, BF),
            sds(fine_shape, BF),
            sds(coarse_shape, BF),
            sds(coarse_shape, BF),
            sds((fine_slots + coarse_slots,), jnp.int32),
            sds((NOP * C, C), BF),
            sds((NOP * C, C), BF),
        ),
        in_specs=[SMEM] + [HBM] * 8,
        out_specs=(HBM, HBM, HBM, HBM, SMEM, HBM, HBM),
        scratch_shapes=[pltpu.VMEM(a.shape, a.dtype) for a in arrays]
        + [
            pltpu.VMEM((fine_boxes, fine_pairs), BF),
            pltpu.VMEM((256, fine_pairs), HOT),
            pltpu.VMEM((coarse_boxes, coarse_pairs), BF),
            pltpu.VMEM((256, coarse_pairs), HOT),
            pltpu.VMEM(fine_shape, BF),
            pltpu.VMEM(fine_shape[1:], BF),
            pltpu.VMEM(coarse_shape, BF),
            pltpu.VMEM(coarse_shape[1:], BF),
            pltpu.VMEM((NOP * C, C), BF),
            pltpu.VMEM((NOP * C, C), BF),
            pltpu.SemaphoreType.DMA((8,)),
            pltpu.SemaphoreType.DMA((fine_slots + coarse_slots + 2,)),
        ],
        cost_estimate=pl.CostEstimate(flops=9_000_000_000, bytes_accessed=8_000_000, transcendentals=0),
        name="counts",
    )(firsts, *arrays)


def place(value, high_part, low_part, rows, lanes):
    high = value.astype(BF)
    high_part[rows, lanes] = high
    low_part[rows, lanes] = (value - high.astype(F32)).astype(BF)


def apply_level(recv, base, slots, n_ref, h_hbm, waits, flag_ref, flag_at, w_ref, w_wait, out_ref, parts, boxes):
    high_part, low_part, total_ref, sem = parts
    lane = lax.broadcasted_iota(jnp.int32, (256, 256), 1)
    many = 512 // boxes
    steps = NOP // (2 * many)

    def sources(slot):
        at = (slot % 2) * 128
        block = recv[:, base : base + 16, at : at + 256].reshape(256, 256).astype(F32)
        turned = pltpu.roll(block, 64 if slot % 2 == 0 else 192, 1)
        left, right = (block, turned) if slot % 2 == 0 else (turned, block)
        return jnp.where(lane < C, left, 0.0).astype(BF), jnp.where(lane >= 64, right, 0.0).astype(BF)

    def split(slot, sides, g):
        start = g * 1024
        at = [pl.ds(start + k * 512 if isinstance(g, int) else pl.multiple_of(start + k * 512, 512), 512) for k in range(2)]
        even = jnp.dot(n_ref[slot, at[0], :], sides[0], preferred_element_type=F32)
        odd = jnp.dot(n_ref[slot, at[1], :], sides[1], preferred_element_type=F32)
        value = jnp.concatenate([even[:, :128], even[:, 128:] + odd[:, :128], odd[:, 128:]], axis=1)
        for k in range(many):
            lanes = (g * many + k) * 2 * C
            lanes = pl.ds(lanes if isinstance(g, int) else pl.multiple_of(lanes, 128), 2 * C)
            rows = slice(slot * boxes, (slot + 1) * boxes)
            place(value[k * boxes : (k + 1) * boxes], high_part, low_part, rows, lanes)

    for slot in range(slots):
        sides = sources(slot)
        for g in range(steps):
            waits[slot][g].wait()
            split(slot, sides, g)
    w_wait.wait()
    w = w_ref[...]
    total = jnp.dot(high_part[...], w, preferred_element_type=F32)
    total_ref[...] = total + jnp.dot(low_part[...], w, preferred_element_type=F32)
    some = flag_ref[flag_at]
    for slot in range(1, slots):
        some = some + flag_ref[flag_at + slot]

    @pl.when(some > 0)
    def _():
        for slot in range(slots):
            rows = slice(slot * boxes, (slot + 1) * boxes)
            high_part[rows, :] = jnp.zeros((boxes, NOP * C), BF)
            low_part[rows, :] = jnp.zeros((boxes, NOP * C), BF)

            @pl.when(flag_ref[flag_at + slot] > 0)
            def _(slot=slot):
                copy = pltpu.make_async_copy(h_hbm.at[slot], n_ref.at[slot], sem)
                copy.start()
                copy.wait()
                sides = sources(slot)
                lax.fori_loop(0, steps, lambda g, _: (split(slot, sides, g), 0)[1], 0)

        def more(k, _):
            at = pl.ds(pl.multiple_of(k * 256, 256), 256)
            extra = jnp.dot(high_part[:, at], w_ref[at, :], preferred_element_type=F32)
            extra = extra + jnp.dot(low_part[:, at], w_ref[at, :], preferred_element_type=F32)
            total_ref[...] = total_ref[...] + 256.0 * extra
            return 0

        lax.fori_loop(0, NOP * C // 256, more, 0)

    for pair in range(slots // 2):
        two = [total_ref[(2 * pair + k) * boxes : (2 * pair + k + 1) * boxes, :] for k in range(2)]
        out_ref[:, pair * 2 * C : (pair + 1) * 2 * C] = jnp.concatenate(two, axis=1).astype(BF)


def apply_kernel(
    flag_ref, recv, fn, fh, cn, ch, fw, cw, fine_out, coarse_out,
    recv_v, fn_v, cn_v, fw_v, cw_v, fine_v, coarse_v, high_part, low_part, total, sems,
):
    fine_slots, coarse_slots = fn.shape[0], cn.shape[0]
    at = 0

    def begin(source, target):
        nonlocal at
        copy = pltpu.make_async_copy(source, target, sems.at[at])
        copy.start()
        at += 1
        return copy

    def chunks(n_ref, n_v, slot):
        rows = [slice(g * 1024, (g + 1) * 1024) for g in range(n_ref.shape[1] // 1024)]
        return [begin(n_ref.at[slot, r, :], n_v.at[slot, r, :]) for r in rows]

    first = begin(recv, recv_v)
    fine_waits = [chunks(fn, fn_v, j) for j in range(fine_slots)]
    fine_w = begin(fw, fw_v)
    coarse_waits = [chunks(cn, cn_v, j) for j in range(coarse_slots)]
    coarse_w = begin(cw, cw_v)
    first.wait()
    parts = (high_part, low_part, total, sems.at[at])
    at += 1
    apply_level(recv_v, 0, fine_slots, fn_v, fh, fine_waits, flag_ref, 0, fw_v, fine_w, fine_v, parts, 128)
    out = begin(fine_v, fine_out)
    apply_level(
        recv_v, 16, coarse_slots, cn_v, ch, coarse_waits, flag_ref, fine_slots, cw_v, coarse_w, coarse_v, parts, 64
    )
    last = begin(coarse_v, coarse_out)
    out.wait()
    last.wait()


def apply(flag, recv, fn, fh, cn, ch, fw, cw, fine_boxes, coarse_boxes):
    rows = fn.shape[0] * fine_boxes
    outs = (
        jax.ShapeDtypeStruct((fine_boxes, fn.shape[0] * C), BF),
        jax.ShapeDtypeStruct((coarse_boxes, cn.shape[0] * C), BF),
    )
    return pl.pallas_call(
        apply_kernel,
        out_shape=outs,
        in_specs=[SMEM] + [HBM] * 7,
        out_specs=(HBM, HBM),
        scratch_shapes=[pltpu.VMEM(a.shape, BF) for a in (recv, fn, cn, fw, cw, *outs)]
        + [
            pltpu.VMEM((rows, NOP * C), BF),
            pltpu.VMEM((rows, NOP * C), BF),
            pltpu.VMEM((rows, C), F32),
            pltpu.SemaphoreType.DMA((24,)),
        ],
        cost_estimate=pl.CostEstimate(flops=3_000_000_000, bytes_accessed=8_000_000, transcendentals=0),
        name="apply",
    )(flag, recv, fn, fh, cn, ch, fw, cw)


def per_device(
    fine_density,
    coarse_density,
    fine_operators,
    coarse_operators,
    fine_balance,
    coarse_balance,
    fine_sources,
    fine_targets,
    fine_op_ids,
    coarse_sources,
    coarse_targets,
    coarse_op_ids,
):
    peers = lax.axis_size("dir")
    count = lax.axis_size("box")
    half = peers // 2
    fine_boxes = fine_density.shape[0] * peers
    coarse_boxes = coarse_density.shape[0] * peers
    position = lax.axis_index("box")
    firsts = jnp.stack([position * fine_boxes, position * coarse_boxes]).astype(jnp.int32)
    route = [(b * peers + d, (b + 1) * peers + d) for b in range(count - 1) for d in range(half, peers)]
    route += [(b * peers + d, (b - 1) * peers + d) for b in range(1, count) for d in range(half)]
    coarse_near = lax.ppermute(coarse_density, ("box", "dir"), route)
    fine_near = lax.ppermute(fine_density, ("box", "dir"), route)
    packed = pack(fine_balance, coarse_balance, fine_density, coarse_density, fine_near, coarse_near, peers)
    firsts, packed = lax.optimization_barrier((firsts, packed))
    recv = lax.all_to_all(packed, "dir", split_axis=0, concat_axis=0, tiled=True)
    fn, fh, cn, ch, flag, fw, cw = counts(
        firsts,
        (fine_sources, fine_targets, fine_op_ids),
        (coarse_sources, coarse_targets, coarse_op_ids),
        fine_operators,
        coarse_operators,
        fine_boxes,
        coarse_boxes,
    )
    return apply(flag, recv, fn, fh, cn, ch, fw, cw, fine_boxes, coarse_boxes)


def solution(mesh):
    placed = (
        P(("box", "dir"), None),
        P(("box", "dir"), None),
        P(),
        P(),
        P(),
        P(),
        P("dir", "box"),
        P("dir", "box"),
        P("dir", "box"),
        P("dir", "box"),
        P("dir", "box"),
        P("dir", "box"),
    )
    return jax.shard_map(
        per_device,
        mesh=mesh,
        in_specs=placed,
        out_specs=(P("box", "dir"), P("box", "dir")),
        check_vma=False,
    )
```

profile of v0, /device:TPU:1, one launch (start us, length us, event | category | flops | bytes accessed | tf_op | source)
XLA Modules:
  0.0 42.2 jit_solution(3567138746342473693)
XLA Ops:
  0.6 8.7 %collective-permute-start = (bf16[8,6144]{1,0:T(8,128)(2,1)}, bf16[8,6144]{1,0:T(8,128)(2,1)S(1)}, u32[]{:S(2)}, u32[]{:S(2)}) collective-permute-start(bf16[8,6144]{1,0:T(8,128)(2,1)} %fd.1), channel_id=1, source_target_pairs={{8,24},{9,25},{10,26},{11,27},{12,28},{13,29},{14,30},{15,31},{24,... | collective-permute-start | bytes 294920 | tf_op jit(solution)/shard_map/ppermute | solution.py:387
  9.4 1.9 %collective-permute-start.1 = (bf16[4,12288]{1,0:T(4,128)(2,1)}, bf16[4,12288]{1,0:T(4,128)(2,1)S(1)}, u32[]{:S(2)}, u32[]{:S(2)}) collective-permute-start(bf16[4,12288]{1,0:T(4,128)(2,1)} %cd.1), channel_id=1, source_target_pairs={{8,24},{9,25},{10,26},{11,27},{12,28},{13,29},{14,30},{15,31},{24,... | collective-permute-start | bytes 294920 | tf_op jit(solution)/shard_map/ppermute | solution.py:386
  11.3 0.6 %pad_add_fusion.firsts = s32[2]{0:T(128)} fusion(s32[1]{0:T(128)} %bitcast.1, s32[1]{0:T(128)} %bitcast), kind=kLoop, calls=%fused_computation | loop fusion | flops 2 | bytes 16 | tf_op jit(solution)/shard_map/stack | solution.py:383
  12.0 0.0 collective-permute-done.fh
  12.0 0.0 copy-start.1
  12.0 3.6 %collective-permute-done.1.ch = bf16[4,12288]{1,0:T(4,128)(2,1)S(1)} collective-permute-done((bf16[4,12288]{1,0:T(4,128)(2,1)}, bf16[4,12288]{1,0:T(4,128)(2,1)S(1)}, u32[]{:S(2)}, u32[]{:S(2)}) %collective-permute-start.1) | collective-permute-done | bytes 98336 | tf_op jit(solution)/shard_map/ppermute | solution.py:386
  15.5 0.0 copy-done.1
  15.5 0.0 copy-start.2
  15.5 0.6 %copy-done.2 = bf16[4,12288]{1,0:T(4,128)(2,1)} copy-done((bf16[4,12288]{1,0:T(4,128)(2,1)}, bf16[4,12288]{1,0:T(4,128)(2,1)S(1)}, u32[]{:S(2)}) %copy-start.2) | copy-done | bytes 98328
  16.2 2.6 %pack.1 = bf16[16,32,384]{2,1,0:T(8,128)(2,1)} custom-call(s32[32]{0:T(128)} %fb.1, s32[64]{0:T(128)} %cb.1, bf16[8,6144]{1,0:T(8,128)(2,1)} %fd.1, bf16[4,12288]{1,0:T(4,128)(2,1)} %cd.1, bf16[8,6144]{1,0:T(8,128)(2,1)} %copy-done.1, bf16[4,12288]{1,0:T(4,128)(2,1)} %copy-done.2), custom_call_target="tpu_custom_call" | custom-call | flops 4000000 | bytes 800000 | tf_op jit(solution)/shard_map/pack/pallas_call | solution.py:77
  18.8 3.6 %all-to-all-start = ((bf16[16,32,384]{2,1,0:T(8,128)(2,1)}), bf16[16,32,384]{2,1,0:T(8,128)(2,1)S(1)}, u32[]{:S(2)}, u32[]{:S(2)}) async-start(bf16[16,32,384]{2,1,0:T(8,128)(2,1)} %pack.1), calls=%async_computation | async-start | bytes 786432 | tf_op jit(solution)/shard_map/all_to_all | solution.py:390
  22.4 9.8 %counts.1 = (bf16[2,2048,256]{2,1,0:T(8,128)(2,1)}, bf16[2,2048,256]{2,1,0:T(8,128)(2,1)}, bf16[4,1024,256]{2,1,0:T(8,128)(2,1)}, bf16[4,1024,256]{2,1,0:T(8,128...) custom-call(s32[2]{0:T(128)} %pad_add_fusion.firsts, s32[2,2048]{1,0:T(2,128)} %fs.1, ...), custom_call_target="tpu_custom_call" | custom-call | flops 8999999488 | bytes 8000000 | tf_op jit(solution)/shard_map/counts/pallas_call | solution.py:198
  32.2 0.0 all-to-all-done.recv
  32.2 0.0 copy-start
  32.2 0.7 %copy-done = bf16[16,32,384]{2,1,0:T(8,128)(2,1)} copy-done((bf16[16,32,384]{2,1,0:T(8,128)(2,1)}, bf16[16,32,384]{2,1,0:T(8,128)(2,1)S(1)}, u32[]{:S(2)}) %copy-start) | copy-done | bytes 393240
  32.9 9.3 %apply.1 = (bf16[128,384]{1,0:T(8,128)(2,1)}, bf16[64,768]{1,0:T(8,128)(2,1)}) custom-call(s32[6]{0:T(128)} %get-tuple-element.12.flag_ref, bf16[16,32,384]{2,1,0:T(8,128)(2,1)} %copy-done, bf16[2,2048,256]{2,1,0:T(8,128)(2,1)} %get-tuple-element.14.fn, bf16[2,2048,256]{2,1,0:T(8,128)(2,1)} %get-tuple-element.15.fh, ...), custom_call_target="tpu_custom_call" | custom-call | flops 3000000000 | bytes 8000000 | tf_op jit(solution)/shard_map/apply/pallas_call | solution.py:346
Async XLA Ops:
  0.6 11.3 %collective-permute-start = (bf16[8,6144]{1,0:T(8,128)(2,1)}, bf16[8,6144]{1,0:T(8,128)(2,1)S(1)}, u32[]{:S(2)}, u32[]{:S(2)}) collective-permute-start(bf16[8,6144]{1,0:T(8,128)(2,1)} %fd.1), channel_id=1, source_target_pairs={{8,24},{9,25},{10,26},{11,27},{12,28},{13,29},{14,30},{15,31},{24,... | collective-permute-start | bytes 294920 | tf_op jit(solution)/shard_map/ppermute | solution.py:387
  9.4 6.1 %collective-permute-start.1 = (bf16[4,12288]{1,0:T(4,128)(2,1)}, bf16[4,12288]{1,0:T(4,128)(2,1)S(1)}, u32[]{:S(2)}, u32[]{:S(2)}) collective-permute-start(bf16[4,12288]{1,0:T(4,128)(2,1)} %cd.1), channel_id=1, source_target_pairs={{8,24},{9,25},{10,26},{11,27},{12,28},{13,29},{14,30},{15,31},{24,... | collective-permute-start | bytes 294920 | tf_op jit(solution)/shard_map/ppermute | solution.py:386
  12.0 3.6 %copy-start.1 = (bf16[8,6144]{1,0:T(8,128)(2,1)}, bf16[8,6144]{1,0:T(8,128)(2,1)S(1)}, u32[]{:S(2)}) copy-start(bf16[8,6144]{1,0:T(8,128)(2,1)S(1)} %collective-permute-done.fh) | copy-start | bytes 294916
  15.5 0.6 %copy-start.2 = (bf16[4,12288]{1,0:T(4,128)(2,1)}, bf16[4,12288]{1,0:T(4,128)(2,1)S(1)}, u32[]{:S(2)}) copy-start(bf16[4,12288]{1,0:T(4,128)(2,1)S(1)} %collective-permute-done.1.ch) | copy-start | bytes 294916
  18.8 13.4 %all-to-all-start = ((bf16[16,32,384]{2,1,0:T(8,128)(2,1)}), bf16[16,32,384]{2,1,0:T(8,128)(2,1)S(1)}, u32[]{:S(2)}, u32[]{:S(2)}) async-start(bf16[16,32,384]{2,1,0:T(8,128)(2,1)} %pack.1), calls=%async_computation | async-start | bytes 786432 | tf_op jit(solution)/shard_map/all_to_all | solution.py:390
  32.2 0.7 %copy-start = (bf16[16,32,384]{2,1,0:T(8,128)(2,1)}, bf16[16,32,384]{2,1,0:T(8,128)(2,1)S(1)}, u32[]{:S(2)}) copy-start(bf16[16,32,384]{2,1,0:T(8,128)(2,1)S(1)} %all-to-all-done.recv) | copy-start | bytes 1179652
where the time goes:
time: 42.5 us; the launch traced here: 42.2 us
  Pallas kernels  21.7 us (51%)
  starting transfers between devices  14.2 us (33%)
  waiting for transfers between devices  3.56 us (8%)
  local copies, waits for them, and re-layouts  1.38 us (3%)
  between operations  0.69 us (2%)
  other arithmetic  0.65 us (2%)
    pallas_call x1, Pallas kernels, counts(): pl.pallas_call(count_kernel, out_shape=(sds(fine_shape, BF), sds(fine_sha...  9.78 us
    pallas_call x1, Pallas kernels, apply(): pl.pallas_call(apply_kernel, out_shape=outs, in_specs=[SMEM] + [HBM] * 7,...  9.3 us
    ppermute x1, starting transfers between devices, per_device(): fine_near = lax.ppermute(fine_density, ('box', 'dir'), route)  8.75 us
    all_to_all x1, starting transfers between devices, per_device(): lax.all_to_all(packed, 'dir', split_axis=0, concat_axis=0, tiled=True)  3.56 us
    ppermute x1, waiting for transfers between devices, per_device(): coarse_near = lax.ppermute(coarse_density, ('box', 'dir'), route)  3.56 us
    pallas_call x1, Pallas kernels, pack(): pl.pallas_call(pack_kernel, out_shape=jax.ShapeDtypeStruct((peers, 32, 2...  2.62 us
    ppermute x1, starting transfers between devices, per_device(): coarse_near = lax.ppermute(coarse_density, ('box', 'dir'), route)  1.92 us
    unnamed x6, local copies, waits for them, and re-layouts  1.38 us
  transfers between devices with their start and end apart: 3, of which 1 were waited for; matrix products, arithmetic and copies ran while one was open for 2% of the time, Pallas kernels for 23%

commit v1 on v0

v1 whole, which is shorter than its diff:
```python
import functools

import jax
import jax.numpy as jnp
from jax import lax
from jax.experimental import pallas as pl
from jax.experimental.pallas import tpu as pltpu
from jax.sharding import PartitionSpec as P

RIM = 32
C = 192
NOP = 16
BF = jnp.bfloat16
F32 = jnp.float32


LIMIT = 50 << 20
BASE = 4096.0
VMEM = pl.BlockSpec(memory_space=pltpu.VMEM)
SMEM = pl.BlockSpec(memory_space=pltpu.SMEM)
HBM = pl.BlockSpec(memory_space=pltpu.HBM)
ANY = pl.BlockSpec(memory_space=pl.ANY)


def fetch(pairs, sems, first=0):
    copies = [pltpu.make_async_copy(s, d, sems.at[first + i]) for i, (s, d) in enumerate(pairs)]
    for copy in copies:
        copy.start()
    return copies


def pack_kernel(fb, cb, fd, cd, fh, ch, out_ref, fb_s, cb_s, fd_v, cd_v, fh_v, ch_v, fine_wide, coarse_wide, sems):
    copies = fetch(((fb, fb_s), (cb, cb_s), (fd, fd_v), (cd, cd_v), (fh, fh_v), (ch, ch_v)), sems)
    for copy in copies:
        copy.wait()
    fine_wide[0:8, :] = fd_v[...].astype(F32)
    fine_wide[8:16, :] = fh_v[...].astype(F32)
    for k, ref in enumerate((cd_v, ch_v)):
        rows = ref[...].astype(F32)
        coarse_wide[8 * k : 8 * k + 4, :] = rows
        coarse_wide[8 * k + 4 : 8 * k + 8, :] = rows
    low = lax.broadcasted_iota(jnp.int32, (16, 128), 1) < 64
    top = (lax.broadcasted_iota(jnp.int32, (16, 128), 0) & 7) < 4

    def window(ref, wedge):
        odd = lax.rem(wedge, 2)
        start = pl.multiple_of(wedge * C - odd * 64, 128)
        first = ref[:, pl.ds(start, 128)]
        second = ref[:, pl.ds(pl.multiple_of(start + 128, 128), 128)]
        return odd == 1, first, second, pltpu.roll(first, 64, 1), pltpu.roll(second, 64, 1)

    def left(ref, wedge):
        odd, first, second, first_r, second_r = window(ref, wedge)
        head = jnp.where(odd, jnp.where(low, first_r, second_r), first)
        return head, jnp.where(odd, second_r, second)

    def right(ref, wedge):
        odd, first, second, first_r, second_r = window(ref, wedge)
        tail = jnp.where(odd, second, jnp.where(low, first_r, second_r))
        return jnp.where(odd, first, first_r), tail

    def joined(even, odd):
        return even[0], jnp.where(low, even[1], odd[0]), odd[1]

    for peer in range(out_ref.shape[0]):
        parts = joined(left(fine_wide, fb_s[2 * peer]), right(fine_wide, fb_s[2 * peer + 1]))
        upper = joined(left(coarse_wide, cb_s[4 * peer]), right(coarse_wide, cb_s[4 * peer + 1]))
        lower = joined(left(coarse_wide, cb_s[4 * peer + 2]), right(coarse_wide, cb_s[4 * peer + 3]))
        for k in range(3):
            lanes = slice(k * 128, (k + 1) * 128)
            out_ref[peer, 0:16, lanes] = parts[k].astype(BF)
            out_ref[peer, 16:32, lanes] = jnp.where(top, upper[k], lower[k]).astype(BF)


def pack(fine_balance, coarse_balance, fine, coarse, fine_near, coarse_near, peers):
    arrays = (fine, coarse, fine_near, coarse_near)
    return pl.pallas_call(
        pack_kernel,
        out_shape=jax.ShapeDtypeStruct((peers, 32, 2 * C), BF),
        in_specs=[HBM] * 4 + [ANY] * 2,
        out_specs=VMEM,
        scratch_shapes=[pltpu.SMEM(fine_balance.shape, jnp.int32), pltpu.SMEM(coarse_balance.shape, jnp.int32)]
        + [pltpu.VMEM(a.shape, BF) for a in arrays]
        + [
            pltpu.VMEM((16, fine.shape[1]), F32),
            pltpu.VMEM((16, coarse.shape[1]), F32),
            pltpu.SemaphoreType.DMA((6,)),
        ],
        cost_estimate=pl.CostEstimate(flops=4_000_000, bytes_accessed=800_000, transcendentals=0),
        name="pack",
    )(fine_balance, coarse_balance, *arrays)


def count_slot(slot, column, src_ref, tgt_ref, op_ref, first, n_ref, h_ref, table, plane, sem, flag_ref, flag_at, tt, st, boxes):
    pairs = src_ref.shape[1]
    rows = lambda v: jnp.broadcast_to(v, (16, pairs))
    steps = lax.broadcasted_iota(jnp.int32, (16, 128), 0).astype(F32)
    one, zero = jnp.ones((), BF), jnp.zeros((), BF)

    def hot(value, block):
        want = jnp.concatenate([(steps + 16.0 * block).astype(BF)] * (pairs // 128), axis=1)
        return jnp.where(value == want, one, zero)

    target = rows(tgt_ref[pl.ds(slot, 1), :] - first).astype(F32).astype(BF)
    source = rows(column(src_ref[pl.ds(slot, 1), :] - first)).astype(F32).astype(BF)
    for k in range(boxes // 16):
        tt[k * 16 : (k + 1) * 16, :] = hot(target, k)
    for k in range(st.shape[0] // 16):
        st[k * 16 : (k + 1) * 16, :] = hot(source, k)
    ops = rows(op_ref[pl.ds(slot, 1), :])
    member = ((ops & 1) * 4 + (ops >> 2)).astype(F32).astype(BF)
    factor = jnp.where((ops & 2) > 0, BASE, 1.0).astype(BF)
    many = 512 // boxes
    wide = st.shape[0] // 128
    planes = 8 // many * wide

    def store(ref, first, g, side, value):
        for k in range(wide):
            ref[first + g * wide + k, side * 512 : (side + 1) * 512, :] = value[:, k * 128 : (k + 1) * 128].astype(BF)

    def count(g):
        parts = []
        for k in range(many):
            mask = jnp.where(member == jnp.asarray(g * many + k, BF), factor, zero)
            part = tt[...].reshape(boxes // 16, 16, pairs) * mask[None]
            parts.append(part.reshape(boxes, pairs))
        lhs = jnp.concatenate(parts, axis=0)
        both = lax.dot_general(lhs, st[...], (((1,), (1,)), ((), ())), preferred_element_type=F32)
        second = jnp.floor(both * (1.0 / BASE))
        return both - second * BASE, second

    most = jnp.float32(0.0)
    for g in range(8 // many):
        found = count(g)
        for side in range(2):
            store(n_ref, plane, g, side, found[side])
        most = jnp.maximum(most, jnp.max(jnp.maximum(found[0], found[1])))
    big = most > 256.0
    flag_ref[pl.ds(flag_at + slot, 1), :] = jnp.full((1, 128), big.astype(F32))

    @pl.when(big)
    def _():
        for g in range(8 // many):
            found = count(g)
            for side in range(2):
                high = jnp.floor(found[side] * (1.0 / 256.0))
                store(n_ref, plane, g, side, found[side] - high * 256.0)
                store(h_ref, 0, g, side, high)
        pltpu.sync_copy(h_ref.at[pl.ds(0, planes)], table.at[pl.ds(n_ref.shape[0] + 1 + plane, planes)])

    pltpu.make_async_copy(n_ref.at[pl.ds(plane, planes)], table.at[pl.ds(plane, planes)], sem).start()


def fine_column(at):
    halo = jnp.logical_or(at < 0, at >= 128).astype(jnp.int32)
    return ((at & 127) >> 3) * 16 + halo * 8 + (at & 7)


def coarse_column(at):
    halo = jnp.logical_or(at < 0, at >= 64).astype(jnp.int32)
    return ((at & 63) >> 2) * 8 + halo * 4 + (at & 3)


def count_kernel(
    firsts, fs, ft, fo, cs, ct, co, table,
    fs_v, ft_v, fo_v, cs_v, ct_v, co_v, ftt, fst, ctt, cst, n_v, h_v, flag_ref, flag_v, sems, out_sems,
):
    copies = fetch(((fs, fs_v), (ft, ft_v), (fo, fo_v), (cs, cs_v), (ct, ct_v), (co, co_v)), sems)
    for copy in copies:
        copy.wait()
    fine_slots, coarse_slots = fs_v.shape[0], cs_v.shape[0]
    last = 4 * fine_slots
    flag_ref[...] = jnp.zeros(flag_ref.shape, F32)

    def fine(j, _):
        index = (fs_v, ft_v, fo_v, firsts[0])
        count_slot(j, fine_column, *index, n_v, h_v, table, 4 * j, out_sems.at[j], flag_ref, 0, ftt, fst, 128)
        return 0

    def coarse(j, _):
        index = (cs_v, ct_v, co_v, firsts[1])
        sem = out_sems.at[fine_slots + j]
        count_slot(j, coarse_column, *index, n_v, h_v, table, last + j, sem, flag_ref, fine_slots, ctt, cst, 64)
        return 0

    lax.fori_loop(0, fine_slots, fine, 0)
    lax.fori_loop(0, coarse_slots, coarse, 0)
    flag_v[...] = flag_ref[...].astype(BF)
    pltpu.sync_copy(flag_v, table.at[n_v.shape[0], 0:16, :])
    for j in range(fine_slots):
        at = pl.ds(4 * j, 4)
        pltpu.make_async_copy(n_v.at[at], table.at[at], out_sems.at[j]).wait()
    for j in range(coarse_slots):
        at = pl.ds(last + j, 1)
        pltpu.make_async_copy(n_v.at[at], table.at[at], out_sems.at[fine_slots + j]).wait()


def counts(firsts, fine_index, coarse_index, fine_boxes, coarse_boxes):
    fine_slots, fine_pairs = fine_index[0].shape
    coarse_slots, coarse_pairs = coarse_index[0].shape
    planes = 4 * fine_slots + coarse_slots
    sds = jax.ShapeDtypeStruct
    arrays = (*fine_index, *coarse_index)
    return pl.pallas_call(
        count_kernel,
        out_shape=sds((2 * planes + 1, 1024, 128), BF),
        in_specs=[SMEM] + [HBM] * 6,
        out_specs=HBM,
        scratch_shapes=[pltpu.VMEM(a.shape, a.dtype) for a in arrays]
        + [
            pltpu.VMEM((fine_boxes, fine_pairs), BF),
            pltpu.VMEM((256, fine_pairs), BF),
            pltpu.VMEM((coarse_boxes, coarse_pairs), BF),
            pltpu.VMEM((128, coarse_pairs), BF),
            pltpu.VMEM((planes, 1024, 128), BF),
            pltpu.VMEM((4, 1024, 128), BF),
            pltpu.VMEM((16, 128), F32),
            pltpu.VMEM((16, 128), BF),
            pltpu.SemaphoreType.DMA((6,)),
            pltpu.SemaphoreType.DMA((fine_slots + coarse_slots,)),
        ],
        cost_estimate=pl.CostEstimate(flops=9_000_000_000, bytes_accessed=8_000_000, transcendentals=0),
        name="counts",
    )(firsts, *arrays)


def apply_level(window, slots, n_ref, table, plane, flag_ref, flag_at, op_ref, out_ref, parts, boxes):
    split_ref, total_ref, waits, flag_wait, sem = parts
    count = slots * boxes
    wide = boxes // 64
    lane = lax.broadcasted_iota(jnp.int32, (128 * wide, 256), 1)
    many = 512 // boxes
    planes = 8 // many * wide
    depth = NOP // 2 * C

    def sources(slot):
        block = window(slot)
        turned = pltpu.roll(block, 64 if slot % 2 == 0 else 192, 1)
        left, right = (block, turned) if slot % 2 == 0 else (turned, block)
        return jnp.where(lane < C, left, 0.0).astype(BF), jnp.where(lane >= 64, right, 0.0).astype(BF)

    def weights(odd):
        start = [odd * 128 + k * 2 * C for k in range(NOP // 2)]
        return jnp.concatenate([op_ref[:, a : a + 256] for a in start], axis=0)

    def split(slot, sides, g):
        at = plane + slot * planes + g * wide
        pick = lambda rows: jnp.concatenate([n_ref[at + k, rows, :] for k in range(wide)], axis=1)
        first = jnp.dot(pick(slice(0, 512)), sides[0], preferred_element_type=F32)
        second = jnp.dot(pick(slice(512, 1024)), sides[1], preferred_element_type=F32)
        value = jnp.concatenate([first[:, :128], first[:, 128:] + second[:, :128], second[:, 128:]], axis=1)
        high = value.astype(BF)
        low = (value - high.astype(F32)).astype(BF)
        for k in range(many):
            lanes = slice((g * many + k) * 2 * C, (g * many + k + 1) * 2 * C)
            rows = slice(k * boxes, (k + 1) * boxes)
            split_ref[slot * boxes : (slot + 1) * boxes, lanes] = high[rows]
            split_ref[count + slot * boxes : count + (slot + 1) * boxes, lanes] = low[rows]

    for slot in range(slots):
        sides = sources(slot)
        for g in range(8 // many):
            waits[plane + slot * planes + g * wide].wait()
            split(slot, sides, g)
    for odd in range(2):
        total = jnp.dot(split_ref[:, odd * depth : (odd + 1) * depth], weights(odd), preferred_element_type=F32)
        total_ref[odd] = total[:count] + total[count:]
    if flag_at == 0:
        flag_wait.wait()

    @pl.when(jnp.max(flag_ref[...].astype(F32)) > 0.0)
    def _():
        for slot in range(slots):
            for first in (slot * boxes, count + slot * boxes):
                split_ref[first : first + boxes, :] = jnp.zeros((boxes, 2 * depth), BF)

            @pl.when(jnp.max(flag_ref[...].astype(F32)[flag_at + slot : flag_at + slot + 1, :]) > 0.0)
            def _(slot=slot):
                at = plane + slot * planes
                copy = pltpu.make_async_copy(
                    table.at[pl.ds(at + n_ref.shape[0] + 1, planes)], n_ref.at[pl.ds(at, planes)], sem
                )
                copy.start()
                copy.wait()
                sides = sources(slot)
                for g in range(8 // many):
                    split(slot, sides, g)

        for odd in range(2):
            extra = jnp.dot(split_ref[:, odd * depth : (odd + 1) * depth], weights(odd), preferred_element_type=F32)
            total_ref[odd] = total_ref[odd] + 256.0 * (extra[:count] + extra[count:])

    low_lanes = lax.broadcasted_iota(jnp.int32, (boxes, 128), 1) < 64
    for pair in range(slots // 2):
        rows = [slice((2 * pair + k) * boxes, (2 * pair + k + 1) * boxes) for k in range(2)]
        left = total_ref[0, rows[0], :] + pltpu.roll(total_ref[1, rows[0], :], 192, 1)
        right = total_ref[1, rows[1], :] + pltpu.roll(total_ref[0, rows[1], :], 64, 1)
        middle = jnp.where(low_lanes, left[:, 128:], right[:, :128])
        for k, piece in enumerate((left[:, :128], middle, right[:, 128:])):
            at = pair * 2 * C + k * 128
            out_ref[:, at : at + 128] = piece.astype(BF)


def apply_kernel(
    recv, table, fop, cop, fine_out, coarse_out, n_v, flag_ref, fine_v, coarse_v, split_ref, total, sems
):
    fine_slots, coarse_slots = fine_out.shape[1] // C, coarse_out.shape[1] // C
    last = 4 * fine_slots
    waits = {}
    for p in [*range(0, last, 2), *range(last, last + coarse_slots)]:
        at = slice(p, p + (2 if p < last else 1))
        waits[p] = pltpu.make_async_copy(table.at[at], n_v.at[at], sems.at[p])
        waits[p].start()
    flag_wait = pltpu.make_async_copy(table.at[n_v.shape[0], 0:16, :], flag_ref, sems.at[1])
    flag_wait.start()
    parts = (split_ref, total, waits, flag_wait, sems.at[5])

    def fine_window(slot):
        at = (slot % 2) * 128
        return recv[:, 0:16, at : at + 256].reshape(256, 256).astype(F32)

    def coarse_window(slot):
        at = (slot % 2) * 128
        own = recv[:, 16:24, at : at + 256].astype(F32)
        halo = recv[:, 24:32, at : at + 256].astype(F32)
        top = lax.broadcasted_iota(jnp.int32, own.shape, 1) < 4
        if slot < 2:
            both = jnp.where(top, own, pltpu.roll(halo, 4, 1))
        else:
            both = jnp.where(top, pltpu.roll(own, 4, 1), halo)
        return both.reshape(128, 256)

    apply_level(fine_window, fine_slots, n_v, table, 0, flag_ref, 0, fop, fine_v, parts, 128)
    done = pltpu.make_async_copy(fine_v, fine_out, sems.at[3])
    done.start()
    apply_level(coarse_window, coarse_slots, n_v, table, last, flag_ref, fine_slots, cop, coarse_v, parts, 64)
    pltpu.sync_copy(coarse_v, coarse_out)
    done.wait()


def apply(recv, table, fine_operators, coarse_operators, fine_shape, coarse_shape):
    rows = fine_shape[0] * fine_shape[1] // C
    outs = (jax.ShapeDtypeStruct(fine_shape, BF), jax.ShapeDtypeStruct(coarse_shape, BF))
    planes = table.shape[0] // 2
    return pl.pallas_call(
        apply_kernel,
        out_shape=outs,
        in_specs=[VMEM, HBM, VMEM, VMEM],
        out_specs=(HBM, HBM),
        scratch_shapes=[
            pltpu.VMEM((planes, 1024, 128), BF),
            pltpu.VMEM((16, 128), BF),
            pltpu.VMEM(fine_shape, BF),
            pltpu.VMEM(coarse_shape, BF),
            pltpu.VMEM((2 * rows, NOP * C), BF),
            pltpu.VMEM((2, rows, 256), F32),
            pltpu.SemaphoreType.DMA((planes,)),
        ],
        compiler_params=pltpu.CompilerParams(vmem_limit_bytes=LIMIT),
        cost_estimate=pl.CostEstimate(flops=3_000_000_000, bytes_accessed=8_000_000, transcendentals=0),
        name="apply",
    )(recv, table, fine_operators, coarse_operators)


def per_device(
    fine_density,
    coarse_density,
    fine_operators,
    coarse_operators,
    fine_balance,
    coarse_balance,
    fine_sources,
    fine_targets,
    fine_op_ids,
    coarse_sources,
    coarse_targets,
    coarse_op_ids,
):
    peers = lax.axis_size("dir")
    count = lax.axis_size("box")
    half = peers // 2
    fine_boxes = fine_density.shape[0] * peers
    coarse_boxes = coarse_density.shape[0] * peers
    position = lax.axis_index("box")
    firsts = jnp.stack([position * fine_boxes, position * coarse_boxes]).astype(jnp.int32)
    route = [(b * peers + d, (b + 1) * peers + d) for b in range(count - 1) for d in range(half, peers)]
    route += [(b * peers + d, (b - 1) * peers + d) for b in range(1, count) for d in range(half)]
    coarse_near = lax.ppermute(coarse_density, ("box", "dir"), route)
    fine_near = lax.ppermute(fine_density, ("box", "dir"), route)
    packed = pack(fine_balance, coarse_balance, fine_density, coarse_density, fine_near, coarse_near, peers)
    firsts, packed = lax.optimization_barrier((firsts, packed))
    recv = lax.all_to_all(packed, "dir", split_axis=0, concat_axis=0, tiled=True)
    table = counts(
        firsts,
        (fine_sources, fine_targets, fine_op_ids),
        (coarse_sources, coarse_targets, coarse_op_ids),
        fine_boxes,
        coarse_boxes,
    )
    fine_shape = (fine_boxes, fine_sources.shape[0] * C)
    coarse_shape = (coarse_boxes, coarse_sources.shape[0] * C)
    return apply(recv, table, fine_operators, coarse_operators, fine_shape, coarse_shape)


def solution(mesh):
    placed = (
        P(("box", "dir"), None),
        P(("box", "dir"), None),
        P(),
        P(),
        P(),
        P(),
        P("dir", "box"),
        P("dir", "box"),
        P("dir", "box"),
        P("dir", "box"),
        P("dir", "box"),
        P("dir", "box"),
    )
    return jax.shard_map(
        per_device,
        mesh=mesh,
        in_specs=placed,
        out_specs=(P("box", "dir"), P("box", "dir")),
        check_vma=False,
    )
```

time: 42.5 us -> 37.2 us (0.88)
  Pallas kernels: 21.7 us -> 16.7 us
  local copies, waits for them, and re-layouts: 1.38 us -> 0.66 us
    pallas_call x2, Pallas kernels: 19.1 us -> 14.1 us  [the longest x1 7.84 us: counts(): pl.pallas_call(count_kernel, out_shape=sds((2 * planes + 1, 1024, 128), B...]
    unnamed x6 -> x8, local copies, waits for them, and re-layouts: 1.38 us -> 0.66 us
  transfers between devices with their start and end apart: 3 -> 3, of which waited for: 1 -> 2; matrix products, arithmetic and copies ran while one was open for 2% -> 2% of each run, Pallas kernels for 23% -> 21%
where the time goes in v1:
time: 37.2 us; the launch traced here: 36.8 us
  Pallas kernels  16.7 us (45%)
  starting transfers between devices  14.2 us (38%)
  waiting for transfers between devices  3.93 us (11%)
  between operations  0.69 us (2%)
  local copies, waits for them, and re-layouts  0.66 us (2%)
  other arithmetic  0.61 us (2%)
    ppermute x1, starting transfers between devices, per_device(): fine_near = lax.ppermute(fine_density, ('box', 'dir'), route)  8.75 us
    pallas_call x1, Pallas kernels, counts(): pl.pallas_call(count_kernel, out_shape=sds((2 * planes + 1, 1024, 128), B...  7.84 us
    pallas_call x1, Pallas kernels, apply(): pl.pallas_call(apply_kernel, out_shape=outs, in_specs=[VMEM, HBM, VMEM, V...  6.21 us
    ppermute x1, waiting for transfers between devices, per_device(): coarse_near = lax.ppermute(coarse_density, ('box', 'dir'), route)  3.59 us
    all_to_all x1, starting transfers between devices, per_device(): lax.all_to_all(packed, 'dir', split_axis=0, concat_axis=0, tiled=True)  3.56 us
    pallas_call x1, Pallas kernels, pack(): pl.pallas_call(pack_kernel, out_shape=jax.ShapeDtypeStruct((peers, 32, 2...  2.64 us
    ppermute x1, starting transfers between devices, per_device(): coarse_near = lax.ppermute(coarse_density, ('box', 'dir'), route)  1.92 us
  transfers between devices with their start and end apart: 3, of which 2 were waited for; matrix products, arithmetic and copies ran while one was open for 2% of the time, Pallas kernels for 21%

profile of v1, /device:TPU:1, one launch (start us, length us, event | category | flops | bytes accessed | tf_op | source)
XLA Modules:
  0.0 36.8 jit_solution(3325917678363076980)
XLA Ops:
  0.6 8.7 %collective-permute-start = (bf16[8,6144]{1,0:T(8,128)(2,1)}, bf16[8,6144]{1,0:T(8,128)(2,1)S(1)}, u32[]{:S(2)}, u32[]{:S(2)}) collective-permute-start(bf16[8,6144]{1,0:T(8,128)(2,1)} %fd.1), channel_id=1, source_target_pairs={{8,24},{9,25},{10,26},{11,27},{12,28},{13,29},{14,30},{15,31},{24,... | collective-permute-start | bytes 294920 | tf_op jit(solution)/shard_map/ppermute | solution.py:389
  9.4 1.9 %collective-permute-start.1 = (bf16[4,12288]{1,0:T(4,128)(2,1)}, bf16[4,12288]{1,0:T(4,128)(2,1)S(1)}, u32[]{:S(2)}, u32[]{:S(2)}) collective-permute-start(bf16[4,12288]{1,0:T(4,128)(2,1)} %cd.1), channel_id=1, source_target_pairs={{8,24},{9,25},{10,26},{11,27},{12,28},{13,29},{14,30},{15,31},{24,... | collective-permute-start | bytes 294920 | tf_op jit(solution)/shard_map/ppermute | solution.py:388
  11.3 0.6 %pad_add_fusion.firsts = s32[2]{0:T(128)} fusion(s32[1]{0:T(128)} %bitcast.1, s32[1]{0:T(128)} %bitcast), kind=kLoop, calls=%fused_computation | loop fusion | flops 2 | bytes 16 | tf_op jit(solution)/shard_map/stack | solution.py:385
  11.9 0.0 collective-permute-done.fh
  11.9 0.0 copy-start.2
  11.9 3.6 %collective-permute-done.1.ch = bf16[4,12288]{1,0:T(4,128)(2,1)S(1)} collective-permute-done((bf16[4,12288]{1,0:T(4,128)(2,1)}, bf16[4,12288]{1,0:T(4,128)(2,1)S(1)}, u32[]{:S(2)}, u32[]{:S(2)}) %collective-permute-start.1) | collective-permute-done | bytes 98336 | tf_op jit(solution)/shard_map/ppermute | solution.py:388
  15.5 0.0 copy-done.2
  15.5 0.0 copy-start.3
  15.5 0.6 %copy-done.3 = bf16[4,12288]{1,0:T(4,128)(2,1)} copy-done((bf16[4,12288]{1,0:T(4,128)(2,1)}, bf16[4,12288]{1,0:T(4,128)(2,1)S(1)}, u32[]{:S(2)}) %copy-start.3) | copy-done | bytes 98328
  16.2 2.6 %pack.1 = bf16[16,32,384]{2,1,0:T(8,128)(2,1)} custom-call(s32[32]{0:T(128)} %fb.1, s32[64]{0:T(128)} %cb.1, bf16[8,6144]{1,0:T(8,128)(2,1)} %fd.1, bf16[4,12288]{1,0:T(4,128)(2,1)} %cd.1, bf16[8,6144]{1,0:T(8,128)(2,1)} %copy-done.2, bf16[4,12288]{1,0:T(4,128)(2,1)} %copy-done.3), custom_call_target="tpu_custom_call" | custom-call | flops 4000000 | bytes 800000 | tf_op jit(solution)/shard_map/pack/pallas_call | solution.py:77
  18.8 3.6 %all-to-all-start = ((bf16[16,32,384]{2,1,0:T(8,128)(2,1)}), bf16[16,32,384]{2,1,0:T(8,128)(2,1)S(1)}, u32[]{:S(2)}, u32[]{:S(2)}) async-start(bf16[16,32,384]{2,1,0:T(8,128)(2,1)} %pack.1), calls=%async_computation | async-start | bytes 786432 | tf_op jit(solution)/shard_map/all_to_all | solution.py:392
  22.4 0.0 copy-start
  22.4 0.0 copy-start.1
  22.4 7.8 %counts.1.table = bf16[25,1024,128]{2,1,0:T(8,128)(2,1)} custom-call(s32[2]{0:T(128)} %pad_add_fusion.firsts, s32[2,2048]{1,0:T(2,128)} %fs.1, s32[2,2048]{1,0:T(2,128)} %ft.1, s32[2,2048]{1,0:T(2,128)} %fo.1, s32[4,1024]{1,0:T(4,128)} %cs.1, s32[4,1024]{1,0:T(4,128)} %ct.1, s32[4,1024]{1,0:T(4,128)} %co.1), custom_call_target="tpu_custom_call" | custom-call | flops 8999999488 | bytes 8000000 | tf_op jit(solution)/shard_map/counts/pallas_call | solution.py:204
  30.3 0.3 all-to-all-done.recv
  30.6 0.0 copy-done
  30.6 0.0 copy-done.1
  30.6 6.2 %apply.1 = (bf16[128,384]{1,0:T(8,128)(2,1)}, bf16[64,768]{1,0:T(8,128)(2,1)}) custom-call(bf16[16,32,384]{2,1,0:T(8,128)(2,1)S(1)} %all-to-all-done.recv, bf16[25,1024,128]{2,1,0:T(8,128)(2,1)} %counts.1.table, bf16[192,3072]{1,0:T(8,128)(2,1)S(1)} %copy-done, bf16[192,3072]{1,0:T(8,128)(2,1)S(1)} %copy-done.1), custom_call_target="tpu_custom_call" | custom-call | flops 3000000000 | bytes 8000000 | tf_op jit(solution)/shard_map/apply/pallas_call | solution.py:345
Async XLA Ops:
  0.6 11.3 %collective-permute-start = (bf16[8,6144]{1,0:T(8,128)(2,1)}, bf16[8,6144]{1,0:T(8,128)(2,1)S(1)}, u32[]{:S(2)}, u32[]{:S(2)}) collective-permute-start(bf16[8,6144]{1,0:T(8,128)(2,1)} %fd.1), channel_id=1, source_target_pairs={{8,24},{9,25},{10,26},{11,27},{12,28},{13,29},{14,30},{15,31},{24,... | collective-permute-start | bytes 294920 | tf_op jit(solution)/shard_map/ppermute | solution.py:389
  9.4 6.1 %collective-permute-start.1 = (bf16[4,12288]{1,0:T(4,128)(2,1)}, bf16[4,12288]{1,0:T(4,128)(2,1)S(1)}, u32[]{:S(2)}, u32[]{:S(2)}) collective-permute-start(bf16[4,12288]{1,0:T(4,128)(2,1)} %cd.1), channel_id=1, source_target_pairs={{8,24},{9,25},{10,26},{11,27},{12,28},{13,29},{14,30},{15,31},{24,... | collective-permute-start | bytes 294920 | tf_op jit(solution)/shard_map/ppermute | solution.py:388
  11.9 3.6 %copy-start.2 = (bf16[8,6144]{1,0:T(8,128)(2,1)}, bf16[8,6144]{1,0:T(8,128)(2,1)S(1)}, u32[]{:S(2)}) copy-start(bf16[8,6144]{1,0:T(8,128)(2,1)S(1)} %collective-permute-done.fh) | copy-start | bytes 294916
  15.5 0.6 %copy-start.3 = (bf16[4,12288]{1,0:T(4,128)(2,1)}, bf16[4,12288]{1,0:T(4,128)(2,1)S(1)}, u32[]{:S(2)}) copy-start(bf16[4,12288]{1,0:T(4,128)(2,1)S(1)} %collective-permute-done.1.ch) | copy-start | bytes 294916
  18.8 11.8 %all-to-all-start = ((bf16[16,32,384]{2,1,0:T(8,128)(2,1)}), bf16[16,32,384]{2,1,0:T(8,128)(2,1)S(1)}, u32[]{:S(2)}, u32[]{:S(2)}) async-start(bf16[16,32,384]{2,1,0:T(8,128)(2,1)} %pack.1), calls=%async_computation | async-start | bytes 786432 | tf_op jit(solution)/shard_map/all_to_all | solution.py:392
  22.4 8.2 %copy-start = (bf16[192,3072]{1,0:T(8,128)(2,1)S(1)}, bf16[192,3072]{1,0:T(8,128)(2,1)}, u32[]{:S(2)}) copy-start(bf16[192,3072]{1,0:T(8,128)(2,1)} %fop.1) | copy-start | bytes 3538948
  22.4 8.2 %copy-start.1 = (bf16[192,3072]{1,0:T(8,128)(2,1)S(1)}, bf16[192,3072]{1,0:T(8,128)(2,1)}, u32[]{:S(2)}) copy-start(bf16[192,3072]{1,0:T(8,128)(2,1)} %cop.1) | copy-start | bytes 3538948

commit v2 on v1

--- a/solution.py
+++ b/solution.py
@@ -15,11 +15,11 @@
 
 
 LIMIT = 50 << 20
+MERGE_LIMIT = 56200000
 BASE = 4096.0
 VMEM = pl.BlockSpec(memory_space=pltpu.VMEM)
 SMEM = pl.BlockSpec(memory_space=pltpu.SMEM)
 HBM = pl.BlockSpec(memory_space=pltpu.HBM)
-ANY = pl.BlockSpec(memory_space=pl.ANY)
 
 
 def fetch(pairs, sems, first=0):
@@ -29,18 +29,16 @@
     return copies
 
 
-def pack_kernel(fb, cb, fd, cd, fh, ch, out_ref, fb_s, cb_s, fd_v, cd_v, fh_v, ch_v, fine_wide, coarse_wide, sems):
-    copies = fetch(((fb, fb_s), (cb, cb_s), (fd, fd_v), (cd, cd_v), (fh, fh_v), (ch, ch_v)), sems)
+def pack_kernel(fb, cb, fd, cd, sorted_ref, packed_ref, fb_s, cb_s, fd_v, cd_v, out_v, fine_wide, coarse_wide, sems):
+    copies = fetch(((fb, fb_s), (cb, cb_s), (fd, fd_v), (cd, cd_v)), sems)
     for copy in copies:
         copy.wait()
-    fine_wide[0:8, :] = fd_v[...].astype(F32)
-    fine_wide[8:16, :] = fh_v[...].astype(F32)
-    for k, ref in enumerate((cd_v, ch_v)):
-        rows = ref[...].astype(F32)
-        coarse_wide[8 * k : 8 * k + 4, :] = rows
-        coarse_wide[8 * k + 4 : 8 * k + 8, :] = rows
-    low = lax.broadcasted_iota(jnp.int32, (16, 128), 1) < 64
-    top = (lax.broadcasted_iota(jnp.int32, (16, 128), 0) & 7) < 4
+    fine_wide[...] = fd_v[...].astype(F32)
+    rows = cd_v[...].astype(F32)
+    coarse_wide[0:4, :] = rows
+    coarse_wide[4:8, :] = rows
+    low = lax.broadcasted_iota(jnp.int32, (8, 128), 1) < 64
+    top = lax.broadcasted_iota(jnp.int32, (8, 128), 0) < 4
 
     def window(ref, wedge):
         odd = lax.rem(wedge, 2)
@@ -62,33 +60,72 @@
     def joined(even, odd):
         return even[0], jnp.where(low, even[1], odd[0]), odd[1]
 
-    for peer in range(out_ref.shape[0]):
+    for peer in range(out_v.shape[0]):
         parts = joined(left(fine_wide, fb_s[2 * peer]), right(fine_wide, fb_s[2 * peer + 1]))
         upper = joined(left(coarse_wide, cb_s[4 * peer]), right(coarse_wide, cb_s[4 * peer + 1]))
         lower = joined(left(coarse_wide, cb_s[4 * peer + 2]), right(coarse_wide, cb_s[4 * peer + 3]))
         for k in range(3):
             lanes = slice(k * 128, (k + 1) * 128)
-            out_ref[peer, 0:16, lanes] = parts[k].astype(BF)
-            out_ref[peer, 16:32, lanes] = jnp.where(top, upper[k], lower[k]).astype(BF)
-
-
-def pack(fine_balance, coarse_balance, fine, coarse, fine_near, coarse_near, peers):
-    arrays = (fine, coarse, fine_near, coarse_near)
+            out_v[peer, 0:8, lanes] = parts[k].astype(BF)
+            out_v[peer, 8:16, lanes] = jnp.where(top, upper[k], lower[k]).astype(BF)
+    copies = fetch(
+        (
+            (out_v, sorted_ref),
+            (out_v.at[:, 0:8, :], packed_ref.at[:, 0:8, :]),
+            (out_v.at[:, 8:16, :], packed_ref.at[:, 16:24, :]),
+        ),
+        sems,
+    )
+    for copy in copies:
+        copy.wait()
+
+
+def pack(fine_balance, coarse_balance, fine, coarse, peers):
+    sds = jax.ShapeDtypeStruct
     return pl.pallas_call(
         pack_kernel,
-        out_shape=jax.ShapeDtypeStruct((peers, 32, 2 * C), BF),
-        in_specs=[HBM] * 4 + [ANY] * 2,
-        out_specs=VMEM,
-        scratch_shapes=[pltpu.SMEM(fine_balance.shape, jnp.int32), pltpu.SMEM(coarse_balance.shape, jnp.int32)]
-        + [pltpu.VMEM(a.shape, BF) for a in arrays]
-        + [
-            pltpu.VMEM((16, fine.shape[1]), F32),
-            pltpu.VMEM((16, coarse.shape[1]), F32),
-            pltpu.SemaphoreType.DMA((6,)),
+        out_shape=(sds((peers, 16, 2 * C), BF), sds((peers, 32, 2 * C), BF)),
+        in_specs=[HBM] * 4,
+        out_specs=(HBM, HBM),
+        scratch_shapes=[
+            pltpu.SMEM(fine_balance.shape, jnp.int32),
+            pltpu.SMEM(coarse_balance.shape, jnp.int32),
+            pltpu.VMEM(fine.shape, BF),
+            pltpu.VMEM(coarse.shape, BF),
+            pltpu.VMEM((peers, 16, 2 * C), BF),
+            pltpu.VMEM((8, fine.shape[1]), F32),
+            pltpu.VMEM((8, coarse.shape[1]), F32),
+            pltpu.SemaphoreType.DMA((4,)),
         ],
         cost_estimate=pl.CostEstimate(flops=4_000_000, bytes_accessed=800_000, transcendentals=0),
         name="pack",
-    )(fine_balance, coarse_balance, *arrays)
+    )(fine_balance, coarse_balance, fine, coarse)
+
+
+def merge_kernel(near, _, packed_ref, sems):
+    copies = fetch(
+        (
+            (near.at[:, 0:8, :], packed_ref.at[:, 8:16, :]),
+            (near.at[:, 8:16, :], packed_ref.at[:, 24:32, :]),
+        ),
+        sems,
+    )
+    for copy in copies:
+        copy.wait()
+
+
+def merge(near, packed):
+    return pl.pallas_call(
+        merge_kernel,
+        out_shape=jax.ShapeDtypeStruct(packed.shape, BF),
+        in_specs=[VMEM, HBM],
+        out_specs=HBM,
+        scratch_shapes=[pltpu.SemaphoreType.DMA((2,))],
+        input_output_aliases={1: 0},
+        compiler_params=pltpu.CompilerParams(vmem_limit_bytes=MERGE_LIMIT),
+        cost_estimate=pl.CostEstimate(flops=0, bytes_accessed=400_000, transcendentals=0),
+        name="merge",
+    )(near, packed)
 
 
 def count_slot(slot, column, src_ref, tgt_ref, op_ref, first, n_ref, h_ref, table, plane, sem, flag_ref, flag_at, tt, st, boxes):
@@ -246,9 +283,15 @@
     def split(slot, sides, g):
         at = plane + slot * planes + g * wide
         pick = lambda rows: jnp.concatenate([n_ref[at + k, rows, :] for k in range(wide)], axis=1)
-        first = jnp.dot(pick(slice(0, 512)), sides[0], preferred_element_type=F32)
-        second = jnp.dot(pick(slice(512, 1024)), sides[1], preferred_element_type=F32)
-        value = jnp.concatenate([first[:, :128], first[:, 128:] + second[:, :128], second[:, 128:]], axis=1)
+        if wide == 1:
+            both = jnp.concatenate([pick(slice(0, 512)), pick(slice(512, 1024))], axis=1)
+            none = jnp.zeros((128, 128), BF)
+            halves = [jnp.concatenate([sides[0], none], axis=1), jnp.concatenate([none, sides[1]], axis=1)]
+            value = jnp.dot(both, jnp.concatenate(halves, axis=0), preferred_element_type=F32)
+        else:
+            first = jnp.dot(pick(slice(0, 512)), sides[0], preferred_element_type=F32)
+            second = jnp.dot(pick(slice(512, 1024)), sides[1], preferred_element_type=F32)
+            value = jnp.concatenate([first[:, :128], first[:, 128:] + second[:, :128], second[:, 128:]], axis=1)
         high = value.astype(BF)
         low = (value - high.astype(F32)).astype(BF)
         for k in range(many):
@@ -385,9 +428,8 @@
     firsts = jnp.stack([position * fine_boxes, position * coarse_boxes]).astype(jnp.int32)
     route = [(b * peers + d, (b + 1) * peers + d) for b in range(count - 1) for d in range(half, peers)]
     route += [(b * peers + d, (b - 1) * peers + d) for b in range(1, count) for d in range(half)]
-    coarse_near = lax.ppermute(coarse_density, ("box", "dir"), route)
-    fine_near = lax.ppermute(fine_density, ("box", "dir"), route)
-    packed = pack(fine_balance, coarse_balance, fine_density, coarse_density, fine_near, coarse_near, peers)
+    mine, packed = pack(fine_balance, coarse_balance, fine_density, coarse_density, peers)
+    packed = merge(lax.ppermute(mine, ("box", "dir"), route), packed)
     firsts, packed = lax.optimization_barrier((firsts, packed))
     recv = lax.all_to_all(packed, "dir", split_axis=0, concat_axis=0, tiled=True)
     table = counts(

time: 37.2 us -> 35.9 us (0.965)
  the two profiles are of different devices: /device:TPU:1 before, /device:TPU:96 now
where the time goes in v2:
time: 35.9 us; the launch traced here: 35.6 us
  Pallas kernels  17.3 us (48%)
  starting transfers between devices  10.8 us (30%)
  waiting for transfers between devices  6.12 us (17%)
  between operations  0.69 us (2%)
  other arithmetic  0.64 us (2%)
    all_to_all x1, starting transfers between devices, per_device(): lax.all_to_all(packed, 'dir', split_axis=0, concat_axis=0, tiled=True)  8.84 us
    pallas_call x1, Pallas kernels, counts(): pl.pallas_call(count_kernel, out_shape=sds((2 * planes + 1, 1024, 128), B...  7.85 us
    pallas_call x1, Pallas kernels, apply(): pl.pallas_call(apply_kernel, out_shape=outs, in_specs=[VMEM, HBM, VMEM, V...  6.26 us
    all_to_all x1, waiting for transfers between devices, per_device(): lax.all_to_all(packed, 'dir', split_axis=0, concat_axis=0, tiled=True)  3.28 us
    ppermute x1, waiting for transfers between devices, per_device(): packed = merge(lax.ppermute(mine, ('box', 'dir'), route), packed)  2.83 us
    pallas_call x1, Pallas kernels, pack(): pl.pallas_call(pack_kernel, out_shape=(sds((peers, 16, 2 * C), BF), sds((...  2.51 us
    ppermute x1, starting transfers between devices, per_device(): packed = merge(lax.ppermute(mine, ('box', 'dir'), route), packed)  1.92 us
    pallas_call x1, Pallas kernels, merge(): pl.pallas_call(merge_kernel, out_shape=jax.ShapeDtypeStruct(packed.shape,...  0.73 us
  transfers between devices with their start and end apart: 2, of which 2 were waited for; matrix products, arithmetic and copies ran while one was open for 2% of the time, Pallas kernels for 22%

profile of v2, /device:TPU:96, one launch (start us, length us, event | category | flops | bytes accessed | tf_op | source)
XLA Modules:
  0.0 35.6 jit_solution(16965819214110626306)
XLA Ops:
  0.6 2.5 %pack.1 = (bf16[16,16,384]{2,1,0:T(8,128)(2,1)}, bf16[16,32,384]{2,1,0:T(8,128)(2,1)}) custom-call(s32[32]{0:T(128)} %fb.1, s32[64]{0:T(128)} %cb.1, bf16[8,6144]{1,0:T(8,128)(2,1)} %fd.1, bf16[4,12288]{1,0:T(4,128)(2,1)} %cd.1), custom_call_target="tpu_custom_call" | custom-call | flops 4000000 | bytes 800000 | tf_op jit(solution)/shard_map/pack/pallas_call | solution.py:85
  3.1 1.9 %collective-permute-start = (bf16[16,16,384]{2,1,0:T(8,128)(2,1)}, bf16[16,16,384]{2,1,0:T(8,128)(2,1)S(1)}, u32[]{:S(2)}, u32[]{:S(2)}) collective-permute-start(bf16[16,16,384]{2,1,0:T(8,128)(2,1)} %get-tuple-element.6), channel_id=1, source_target_pairs={{8,24},{9,25},{10,26},{11,27},{12,28},{13,29},{14,30},{15,31},{24,... | collective-permute-start | bytes 589832 | tf_op jit(solution)/shard_map/ppermute | solution.py:432
  5.1 0.6 %pad_add_fusion.firsts = s32[2]{0:T(128)} fusion(s32[1]{0:T(128)} %bitcast.1, s32[1]{0:T(128)} %bitcast), kind=kLoop, calls=%fused_computation | loop fusion | flops 2 | bytes 16 | tf_op jit(solution)/shard_map/stack | solution.py:428
  5.7 2.8 %collective-permute-done.near = bf16[16,16,384]{2,1,0:T(8,128)(2,1)S(1)} collective-permute-done((bf16[16,16,384]{2,1,0:T(8,128)(2,1)}, bf16[16,16,384]{2,1,0:T(8,128)(2,1)S(1)}, u32[]{:S(2)}, u32[]{:S(2)}) %collective-permute-start) | collective-permute-done | bytes 196640 | tf_op jit(solution)/shard_map/ppermute | solution.py:432
  8.6 0.7 %merge.1 = bf16[16,32,384]{2,1,0:T(8,128)(2,1)} custom-call(bf16[16,16,384]{2,1,0:T(8,128)(2,1)S(1)} %collective-permute-done.near, bf16[16,32,384]{2,1,0:T(8,128)(2,1)} %get-tuple-element.7._), custom_call_target="tpu_custom_call", output_to_operand_aliasing={{}: (1, {})} | custom-call | bytes 400000 | tf_op jit(solution)/shard_map/merge/pallas_call | solution.py:118
  9.3 8.8 %all-to-all-start = ((bf16[16,32,384]{2,1,0:T(8,128)(2,1)}), bf16[16,32,384]{2,1,0:T(8,128)(2,1)S(1)}, u32[]{:S(2)}, u32[]{:S(2)}) async-start(bf16[16,32,384]{2,1,0:T(8,128)(2,1)} %merge.1), calls=%async_computation | async-start | bytes 786432 | tf_op jit(solution)/shard_map/all_to_all | solution.py:434
  18.1 0.0 copy-start
  18.1 0.0 copy-start.1
  18.2 7.8 %counts.1.table = bf16[25,1024,128]{2,1,0:T(8,128)(2,1)} custom-call(s32[2]{0:T(128)} %pad_add_fusion.firsts, s32[2,2048]{1,0:T(2,128)} %fs.1, s32[2,2048]{1,0:T(2,128)} %ft.1, s32[2,2048]{1,0:T(2,128)} %fo.1, s32[4,1024]{1,0:T(4,128)} %cs.1, s32[4,1024]{1,0:T(4,128)} %ct.1, s32[4,1024]{1,0:T(4,128)} %co.1), custom_call_target="tpu_custom_call" | custom-call | flops 8999999488 | bytes 8000000 | tf_op jit(solution)/shard_map/counts/pallas_call | solution.py:241
  26.0 3.3 %all-to-all-done.recv = bf16[16,32,384]{2,1,0:T(8,128)(2,1)S(1)} async-done(((bf16[16,32,384]{2,1,0:T(8,128)(2,1)}), bf16[16,32,384]{2,1,0:T(8,128)(2,1)S(1)}, u32[]{:S(2)}, u32[]{:S(2)}) %all-to-all-start) | async-done | bytes 393248 | tf_op jit(solution)/shard_map/all_to_all | solution.py:434
  29.3 0.0 copy-done
  29.3 0.0 copy-done.1
  29.3 6.3 %apply.1 = (bf16[128,384]{1,0:T(8,128)(2,1)}, bf16[64,768]{1,0:T(8,128)(2,1)}) custom-call(bf16[16,32,384]{2,1,0:T(8,128)(2,1)S(1)} %all-to-all-done.recv, bf16[25,1024,128]{2,1,0:T(8,128)(2,1)} %counts.1.table, bf16[192,3072]{1,0:T(8,128)(2,1)S(1)} %copy-done, bf16[192,3072]{1,0:T(8,128)(2,1)S(1)} %copy-done.1), custom_call_target="tpu_custom_call" | custom-call | flops 3000000000 | bytes 8000000 | tf_op jit(solution)/shard_map/apply/pallas_call | solution.py:388
Async XLA Ops:
  3.1 5.4 %collective-permute-start = (bf16[16,16,384]{2,1,0:T(8,128)(2,1)}, bf16[16,16,384]{2,1,0:T(8,128)(2,1)S(1)}, u32[]{:S(2)}, u32[]{:S(2)}) collective-permute-start(bf16[16,16,384]{2,1,0:T(8,128)(2,1)} %get-tuple-element.6), channel_id=1, source_target_pairs={{8,24},{9,25},{10,26},{11,27},{12,28},{13,29},{14,30},{15,31},{24,... | collective-permute-start | bytes 589832 | tf_op jit(solution)/shard_map/ppermute | solution.py:432
  9.3 20.0 %all-to-all-start = ((bf16[16,32,384]{2,1,0:T(8,128)(2,1)}), bf16[16,32,384]{2,1,0:T(8,128)(2,1)S(1)}, u32[]{:S(2)}, u32[]{:S(2)}) async-start(bf16[16,32,384]{2,1,0:T(8,128)(2,1)} %merge.1), calls=%async_computation | async-start | bytes 786432 | tf_op jit(solution)/shard_map/all_to_all | solution.py:434
  18.1 11.2 %copy-start = (bf16[192,3072]{1,0:T(8,128)(2,1)S(1)}, bf16[192,3072]{1,0:T(8,128)(2,1)}, u32[]{:S(2)}) copy-start(bf16[192,3072]{1,0:T(8,128)(2,1)} %fop.1) | copy-start | bytes 3538948
  18.1 11.2 %copy-start.1 = (bf16[192,3072]{1,0:T(8,128)(2,1)S(1)}, bf16[192,3072]{1,0:T(8,128)(2,1)}, u32[]{:S(2)}) copy-start(bf16[192,3072]{1,0:T(8,128)(2,1)} %cop.1) | copy-start | bytes 3538948

commit v3 on v2

--- a/solution.py
+++ b/solution.py
@@ -30,13 +30,7 @@
 
 
 def pack_kernel(fb, cb, fd, cd, sorted_ref, packed_ref, fb_s, cb_s, fd_v, cd_v, out_v, fine_wide, coarse_wide, sems):
-    copies = fetch(((fb, fb_s), (cb, cb_s), (fd, fd_v), (cd, cd_v)), sems)
-    for copy in copies:
-        copy.wait()
-    fine_wide[...] = fd_v[...].astype(F32)
-    rows = cd_v[...].astype(F32)
-    coarse_wide[0:4, :] = rows
-    coarse_wide[4:8, :] = rows
+    copies = fetch(((fb, fb_s), (fd, fd_v), (cb, cb_s), (cd, cd_v)), sems)
     low = lax.broadcasted_iota(jnp.int32, (8, 128), 1) < 64
     top = lax.broadcasted_iota(jnp.int32, (8, 128), 0) < 4
 
@@ -60,23 +54,33 @@
     def joined(even, odd):
         return even[0], jnp.where(low, even[1], odd[0]), odd[1]
 
-    for peer in range(out_v.shape[0]):
+    peers = out_v.shape[0]
+    for copy in copies[:2]:
+        copy.wait()
+    fine_wide[...] = fd_v[...].astype(F32)
+    for peer in range(peers):
         parts = joined(left(fine_wide, fb_s[2 * peer]), right(fine_wide, fb_s[2 * peer + 1]))
-        upper = joined(left(coarse_wide, cb_s[4 * peer]), right(coarse_wide, cb_s[4 * peer + 1]))
-        lower = joined(left(coarse_wide, cb_s[4 * peer + 2]), right(coarse_wide, cb_s[4 * peer + 3]))
         for k in range(3):
-            lanes = slice(k * 128, (k + 1) * 128)
-            out_v[peer, 0:8, lanes] = parts[k].astype(BF)
-            out_v[peer, 8:16, lanes] = jnp.where(top, upper[k], lower[k]).astype(BF)
-    copies = fetch(
-        (
-            (out_v, sorted_ref),
-            (out_v.at[:, 0:8, :], packed_ref.at[:, 0:8, :]),
-            (out_v.at[:, 8:16, :], packed_ref.at[:, 16:24, :]),
-        ),
-        sems,
-    )
-    for copy in copies:
+            out_v[peer, 0:8, k * 128 : (k + 1) * 128] = parts[k].astype(BF)
+    rows = slice(0, 8)
+    fine_rows = out_v.at[:, rows, :]
+    sent = fetch(((fine_rows, sorted_ref.at[:, rows, :]), (fine_rows, packed_ref.at[:, rows, :])), sems, 4)
+    for copy in copies[2:]:
+        copy.wait()
+    coarse_half = cd_v[...].astype(F32)
+    coarse_wide[0:4, :] = coarse_half
+    coarse_wide[4:8, :] = coarse_half
+    for group in range(0, peers, 4):
+        for peer in range(group, group + 4):
+            upper = joined(left(coarse_wide, cb_s[4 * peer]), right(coarse_wide, cb_s[4 * peer + 1]))
+            lower = joined(left(coarse_wide, cb_s[4 * peer + 2]), right(coarse_wide, cb_s[4 * peer + 3]))
+            for k in range(3):
+                out_v[peer, 8:16, k * 128 : (k + 1) * 128] = jnp.where(top, upper[k], lower[k]).astype(BF)
+        at = slice(group, group + 4)
+        half = out_v.at[at, 8:16, :]
+        pair = ((half, sorted_ref.at[at, 8:16, :]), (half, packed_ref.at[at, 16:24, :]))
+        sent += fetch(pair, sems, 6 + group // 2)
+    for copy in sent:
         copy.wait()
 
 
@@ -95,7 +99,7 @@
             pltpu.VMEM((peers, 16, 2 * C), BF),
             pltpu.VMEM((8, fine.shape[1]), F32),
             pltpu.VMEM((8, coarse.shape[1]), F32),
-            pltpu.SemaphoreType.DMA((4,)),
+            pltpu.SemaphoreType.DMA((14,)),
         ],
         cost_estimate=pl.CostEstimate(flops=4_000_000, bytes_accessed=800_000, transcendentals=0),
         name="pack",
@@ -261,29 +265,34 @@
     )(firsts, *arrays)
 
 
-def apply_level(window, slots, n_ref, table, plane, flag_ref, flag_at, op_ref, out_ref, parts, boxes):
-    split_ref, total_ref, waits, flag_wait, sem = parts
-    count = slots * boxes
-    wide = boxes // 64
-    lane = lax.broadcasted_iota(jnp.int32, (128 * wide, 256), 1)
-    many = 512 // boxes
-    planes = 8 // many * wide
-    depth = NOP // 2 * C
-
-    def sources(slot):
-        block = window(slot)
+class Level:
+    def __init__(self, window, n_ref, plane, flag_ref, flag_at, table, op_ref, out_ref, split_ref, total_ref, boxes):
+        self.window, self.n_ref, self.plane, self.table = window, n_ref, plane, table
+        self.flag_ref, self.flag_at = flag_ref, flag_at
+        self.op_ref, self.out_ref, self.split_ref, self.total_ref = op_ref, out_ref, split_ref, total_ref
+        self.boxes = boxes
+        self.count = split_ref.shape[0] // 2
+        self.slots = self.count // boxes
+        self.wide = boxes // 64
+        self.many = 512 // boxes
+        self.planes = 8 // self.many * self.wide
+        self.depth = NOP // 2 * C
+
+    def sources(self, slot):
+        lane = lax.broadcasted_iota(jnp.int32, (128 * self.wide, 256), 1)
+        block = self.window(slot)
         turned = pltpu.roll(block, 64 if slot % 2 == 0 else 192, 1)
         left, right = (block, turned) if slot % 2 == 0 else (turned, block)
         return jnp.where(lane < C, left, 0.0).astype(BF), jnp.where(lane >= 64, right, 0.0).astype(BF)
 
-    def weights(odd):
+    def weights(self, odd):
         start = [odd * 128 + k * 2 * C for k in range(NOP // 2)]
-        return jnp.concatenate([op_ref[:, a : a + 256] for a in start], axis=0)
-
-    def split(slot, sides, g):
-        at = plane + slot * planes + g * wide
-        pick = lambda rows: jnp.concatenate([n_ref[at + k, rows, :] for k in range(wide)], axis=1)
-        if wide == 1:
+        return jnp.concatenate([self.op_ref[:, a : a + 256] for a in start], axis=0)
+
+    def split(self, slot, sides, ref, plane, g):
+        at = plane + g * self.wide
+        pick = lambda rows: jnp.concatenate([ref[at + k, rows, :] for k in range(self.wide)], axis=1)
+        if self.wide == 1:
             both = jnp.concatenate([pick(slice(0, 512)), pick(slice(512, 1024))], axis=1)
             none = jnp.zeros((128, 128), BF)
             halves = [jnp.concatenate([sides[0], none], axis=1), jnp.concatenate([none, sides[1]], axis=1)]
@@ -294,69 +303,80 @@
             value = jnp.concatenate([first[:, :128], first[:, 128:] + second[:, :128], second[:, 128:]], axis=1)
         high = value.astype(BF)
         low = (value - high.astype(F32)).astype(BF)
+        many, boxes = self.many, self.boxes
         for k in range(many):
             lanes = slice((g * many + k) * 2 * C, (g * many + k + 1) * 2 * C)
             rows = slice(k * boxes, (k + 1) * boxes)
-            split_ref[slot * boxes : (slot + 1) * boxes, lanes] = high[rows]
-            split_ref[count + slot * boxes : count + (slot + 1) * boxes, lanes] = low[rows]
-
-    for slot in range(slots):
-        sides = sources(slot)
-        for g in range(8 // many):
-            waits[plane + slot * planes + g * wide].wait()
-            split(slot, sides, g)
-    for odd in range(2):
-        total = jnp.dot(split_ref[:, odd * depth : (odd + 1) * depth], weights(odd), preferred_element_type=F32)
-        total_ref[odd] = total[:count] + total[count:]
-    if flag_at == 0:
-        flag_wait.wait()
-
-    @pl.when(jnp.max(flag_ref[...].astype(F32)) > 0.0)
-    def _():
-        for slot in range(slots):
-            for first in (slot * boxes, count + slot * boxes):
-                split_ref[first : first + boxes, :] = jnp.zeros((boxes, 2 * depth), BF)
-
-            @pl.when(jnp.max(flag_ref[...].astype(F32)[flag_at + slot : flag_at + slot + 1, :]) > 0.0)
-            def _(slot=slot):
-                at = plane + slot * planes
-                copy = pltpu.make_async_copy(
-                    table.at[pl.ds(at + n_ref.shape[0] + 1, planes)], n_ref.at[pl.ds(at, planes)], sem
-                )
-                copy.start()
-                copy.wait()
-                sides = sources(slot)
-                for g in range(8 // many):
-                    split(slot, sides, g)
-
+            self.split_ref[slot * boxes : (slot + 1) * boxes, lanes] = high[rows]
+            self.split_ref[self.count + slot * boxes : self.count + (slot + 1) * boxes, lanes] = low[rows]
+
+    def gather(self, waits):
+        for slot in range(self.slots):
+            sides = self.sources(slot)
+            for g in range(8 // self.many):
+                if waits:
+                    waits[slot * 8 // self.many + g].wait()
+                self.split(slot, sides, self.n_ref, self.plane + slot * self.planes, g)
+
+    def operate(self, odd):
+        at = slice(odd * self.depth, (odd + 1) * self.depth)
+        total = jnp.dot(self.split_ref[:, at], self.weights(odd), preferred_element_type=F32)
+        return total[: self.count] + total[self.count :]
+
+    def translate(self):
         for odd in range(2):
-            extra = jnp.dot(split_ref[:, odd * depth : (odd + 1) * depth], weights(odd), preferred_element_type=F32)
-            total_ref[odd] = total_ref[odd] + 256.0 * (extra[:count] + extra[count:])
-
-    low_lanes = lax.broadcasted_iota(jnp.int32, (boxes, 128), 1) < 64
-    for pair in range(slots // 2):
-        rows = [slice((2 * pair + k) * boxes, (2 * pair + k + 1) * boxes) for k in range(2)]
-        left = total_ref[0, rows[0], :] + pltpu.roll(total_ref[1, rows[0], :], 192, 1)
-        right = total_ref[1, rows[1], :] + pltpu.roll(total_ref[0, rows[1], :], 64, 1)
-        middle = jnp.where(low_lanes, left[:, 128:], right[:, :128])
-        for k, piece in enumerate((left[:, :128], middle, right[:, 128:])):
-            at = pair * 2 * C + k * 128
-            out_ref[:, at : at + 128] = piece.astype(BF)
+            self.total_ref[odd] = self.operate(odd)
+
+    def add_high(self, h_v, sem):
+        boxes, planes = self.boxes, self.planes
+
+        flags = slice(self.flag_at, self.flag_at + self.slots)
+
+        @pl.when(jnp.max(self.flag_ref[...].astype(F32)[flags]) > 0.0)
+        def _():
+            for slot in range(self.slots):
+                for first in (slot * boxes, self.count + slot * boxes):
+                    self.split_ref[first : first + boxes, :] = jnp.zeros((boxes, 2 * self.depth), BF)
+
+                at = self.flag_at + slot
+
+                @pl.when(jnp.max(self.flag_ref[...].astype(F32)[at : at + 1, :]) > 0.0)
+                def _(slot=slot):
+                    first = self.n_ref.shape[0] + 1 + self.plane + slot * planes
+                    copy = pltpu.make_async_copy(self.table.at[pl.ds(first, planes)], h_v.at[pl.ds(0, planes)], sem)
+                    copy.start()
+                    copy.wait()
+                    sides = self.sources(slot)
+                    for g in range(8 // self.many):
+                        self.split(slot, sides, h_v, 0, g)
+
+            for odd in range(2):
+                self.total_ref[odd] = self.total_ref[odd] + 256.0 * self.operate(odd)
+
+    def finish(self):
+        boxes = self.boxes
+        low_lanes = lax.broadcasted_iota(jnp.int32, (boxes, 128), 1) < 64
+        for pair in range(self.slots // 2):
+            rows = [slice((2 * pair + k) * boxes, (2 * pair + k + 1) * boxes) for k in range(2)]
+            left = self.total_ref[0, rows[0], :] + pltpu.roll(self.total_ref[1, rows[0], :], 192, 1)
+            right = self.total_ref[1, rows[1], :] + pltpu.roll(self.total_ref[0, rows[1], :], 64, 1)
+            middle = jnp.where(low_lanes, left[:, 128:], right[:, :128])
+            for k, piece in enumerate((left[:, :128], middle, right[:, 128:])):
+                at = pair * 2 * C + k * 128
+                self.out_ref[:, at : at + 128] = piece.astype(BF)
 
 
 def apply_kernel(
-    recv, table, fop, cop, fine_out, coarse_out, n_v, flag_ref, fine_v, coarse_v, split_ref, total, sems
+    recv, table, fop, cop, fine_out, coarse_out,
+    n_v, flag_v, fine_o, coarse_o, fine_split, coarse_split, fine_total, coarse_total, h_v, sems,
 ):
     fine_slots, coarse_slots = fine_out.shape[1] // C, coarse_out.shape[1] // C
     last = 4 * fine_slots
-    waits = {}
-    for p in [*range(0, last, 2), *range(last, last + coarse_slots)]:
-        at = slice(p, p + (2 if p < last else 1))
-        waits[p] = pltpu.make_async_copy(table.at[at], n_v.at[at], sems.at[p])
-        waits[p].start()
-    flag_wait = pltpu.make_async_copy(table.at[n_v.shape[0], 0:16, :], flag_ref, sems.at[1])
-    flag_wait.start()
-    parts = (split_ref, total, waits, flag_wait, sems.at[5])
+    pieces = [slice(p, p + 2) for p in range(0, last, 2)]
+    fine_waits = fetch([(table.at[p], n_v.at[p]) for p in pieces], sems, 2)
+    tail = slice(last, last + coarse_slots)
+    rest = [(table.at[n_v.shape[0], 0:16, :], flag_v), (table.at[tail], n_v.at[tail])]
+    rest = fetch(rest, sems, 2 + len(pieces))
 
     def fine_window(slot):
         at = (slot % 2) * 128
@@ -373,11 +393,22 @@
             both = jnp.where(top, pltpu.roll(own, 4, 1), halo)
         return both.reshape(128, 256)
 
-    apply_level(fine_window, fine_slots, n_v, table, 0, flag_ref, 0, fop, fine_v, parts, 128)
-    done = pltpu.make_async_copy(fine_v, fine_out, sems.at[3])
+    ends = ((fine_o, fine_split, fine_total, 128), (coarse_o, coarse_split, coarse_total, 64))
+    fine = Level(fine_window, n_v, 0, flag_v, 0, table, fop, *ends[0])
+    coarse = Level(coarse_window, n_v, last, flag_v, fine_slots, table, cop, *ends[1])
+    fine.gather(fine_waits)
+    for copy in rest:
+        copy.wait()
+    fine.translate()
+    coarse.gather([])
+    coarse.translate()
+    fine.add_high(h_v, sems.at[0])
+    coarse.add_high(h_v, sems.at[0])
+    fine.finish()
+    done = pltpu.make_async_copy(fine_o, fine_out, sems.at[1])
     done.start()
-    apply_level(coarse_window, coarse_slots, n_v, table, last, flag_ref, fine_slots, cop, coarse_v, parts, 64)
-    pltpu.sync_copy(coarse_v, coarse_out)
+    coarse.finish()
+    pltpu.sync_copy(coarse_o, coarse_out)
     done.wait()
 
 
@@ -396,8 +427,11 @@
             pltpu.VMEM(fine_shape, BF),
             pltpu.VMEM(coarse_shape, BF),
             pltpu.VMEM((2 * rows, NOP * C), BF),
+            pltpu.VMEM((2 * rows, NOP * C), BF),
             pltpu.VMEM((2, rows, 256), F32),
-            pltpu.SemaphoreType.DMA((planes,)),
+            pltpu.VMEM((2, rows, 256), F32),
+            pltpu.VMEM((4, 1024, 128), BF),
+            pltpu.SemaphoreType.DMA((8,)),
         ],
         compiler_params=pltpu.CompilerParams(vmem_limit_bytes=LIMIT),
         cost_estimate=pl.CostEstimate(flops=3_000_000_000, bytes_accessed=8_000_000, transcendentals=0),

time: 35.9 us -> 35.2 us (0.981)
  Pallas kernels: 17.3 us -> 16.6 us
    pallas_call x1, Pallas kernels: 6.26 us -> 5.64 us  [apply(): pl.pallas_call(apply_kernel, out_shape=outs, in_specs=[VMEM, HBM, VMEM, V...]
where the time goes in v3:
time: 35.2 us; the launch traced here: 34.9 us
  Pallas kernels  16.6 us (47%)
  starting transfers between devices  10.8 us (31%)
  waiting for transfers between devices  6.12 us (17%)
  between operations  0.69 us (2%)
  other arithmetic  0.64 us (2%)
    all_to_all x1, starting transfers between devices, per_device(): lax.all_to_all(packed, 'dir', split_axis=0, concat_axis=0, tiled=True)  8.84 us
    pallas_call x1, Pallas kernels, counts(): pl.pallas_call(count_kernel, out_shape=sds((2 * planes + 1, 1024, 128), B...  7.85 us
    pallas_call x1, Pallas kernels, apply(): pl.pallas_call(apply_kernel, out_shape=outs, in_specs=[VMEM, HBM, VMEM, V...  5.64 us
    all_to_all x1, waiting for transfers between devices, per_device(): lax.all_to_all(packed, 'dir', split_axis=0, concat_axis=0, tiled=True)  3.28 us
    ppermute x1, waiting for transfers between devices, per_device(): packed = merge(lax.ppermute(mine, ('box', 'dir'), route), packed)  2.83 us
    pallas_call x1, Pallas kernels, pack(): pl.pallas_call(pack_kernel, out_shape=(sds((peers, 16, 2 * C), BF), sds((...  2.42 us
    ppermute x1, starting transfers between devices, per_device(): packed = merge(lax.ppermute(mine, ('box', 'dir'), route), packed)  1.92 us
    pallas_call x1, Pallas kernels, merge(): pl.pallas_call(merge_kernel, out_shape=jax.ShapeDtypeStruct(packed.shape,...  0.73 us
  transfers between devices with their start and end apart: 2, of which 2 were waited for; matrix products, arithmetic and copies ran while one was open for 2% of the time, Pallas kernels for 22%

profile of v3, /device:TPU:96, one launch (start us, length us, event | category | flops | bytes accessed | tf_op | source)
XLA Modules:
  0.0 34.9 jit_solution(12136815492491753435)
XLA Ops:
  0.6 2.4 %pack.1 = (bf16[16,16,384]{2,1,0:T(8,128)(2,1)}, bf16[16,32,384]{2,1,0:T(8,128)(2,1)}) custom-call(s32[32]{0:T(128)} %fb.1, s32[64]{0:T(128)} %cb.1, bf16[8,6144]{1,0:T(8,128)(2,1)} %fd.1, bf16[4,12288]{1,0:T(4,128)(2,1)} %cd.1), custom_call_target="tpu_custom_call" | custom-call | flops 4000000 | bytes 800000 | tf_op jit(solution)/shard_map/pack/pallas_call | solution.py:89
  3.1 1.9 %collective-permute-start = (bf16[16,16,384]{2,1,0:T(8,128)(2,1)}, bf16[16,16,384]{2,1,0:T(8,128)(2,1)S(1)}, u32[]{:S(2)}, u32[]{:S(2)}) collective-permute-start(bf16[16,16,384]{2,1,0:T(8,128)(2,1)} %get-tuple-element.6), channel_id=1, source_target_pairs={{8,24},{9,25},{10,26},{11,27},{12,28},{13,29},{14,30},{15,31},{24,... | collective-permute-start | bytes 589832 | tf_op jit(solution)/shard_map/ppermute | solution.py:466
  5.0 0.6 %pad_add_fusion.firsts = s32[2]{0:T(128)} fusion(s32[1]{0:T(128)} %bitcast.1, s32[1]{0:T(128)} %bitcast), kind=kLoop, calls=%fused_computation | loop fusion | flops 2 | bytes 16 | tf_op jit(solution)/shard_map/stack | solution.py:462
  5.6 2.8 %collective-permute-done.near = bf16[16,16,384]{2,1,0:T(8,128)(2,1)S(1)} collective-permute-done((bf16[16,16,384]{2,1,0:T(8,128)(2,1)}, bf16[16,16,384]{2,1,0:T(8,128)(2,1)S(1)}, u32[]{:S(2)}, u32[]{:S(2)}) %collective-permute-start) | collective-permute-done | bytes 196640 | tf_op jit(solution)/shard_map/ppermute | solution.py:466
  8.5 0.7 %merge.1 = bf16[16,32,384]{2,1,0:T(8,128)(2,1)} custom-call(bf16[16,16,384]{2,1,0:T(8,128)(2,1)S(1)} %collective-permute-done.near, bf16[16,32,384]{2,1,0:T(8,128)(2,1)} %get-tuple-element.7._), custom_call_target="tpu_custom_call", output_to_operand_aliasing={{}: (1, {})} | custom-call | bytes 400000 | tf_op jit(solution)/shard_map/merge/pallas_call | solution.py:122
  9.2 8.8 %all-to-all-start = ((bf16[16,32,384]{2,1,0:T(8,128)(2,1)}), bf16[16,32,384]{2,1,0:T(8,128)(2,1)S(1)}, u32[]{:S(2)}, u32[]{:S(2)}) async-start(bf16[16,32,384]{2,1,0:T(8,128)(2,1)} %merge.1), calls=%async_computation | async-start | bytes 786432 | tf_op jit(solution)/shard_map/all_to_all | solution.py:468
  18.0 0.0 copy-start
  18.1 0.0 copy-start.1
  18.1 7.8 %counts.1.table = bf16[25,1024,128]{2,1,0:T(8,128)(2,1)} custom-call(s32[2]{0:T(128)} %pad_add_fusion.firsts, s32[2,2048]{1,0:T(2,128)} %fs.1, s32[2,2048]{1,0:T(2,128)} %ft.1, s32[2,2048]{1,0:T(2,128)} %fo.1, s32[4,1024]{1,0:T(4,128)} %cs.1, s32[4,1024]{1,0:T(4,128)} %ct.1, s32[4,1024]{1,0:T(4,128)} %co.1), custom_call_target="tpu_custom_call" | custom-call | flops 8999999488 | bytes 8000000 | tf_op jit(solution)/shard_map/counts/pallas_call | solution.py:245
  25.9 3.3 %all-to-all-done.recv = bf16[16,32,384]{2,1,0:T(8,128)(2,1)S(1)} async-done(((bf16[16,32,384]{2,1,0:T(8,128)(2,1)}), bf16[16,32,384]{2,1,0:T(8,128)(2,1)S(1)}, u32[]{:S(2)}, u32[]{:S(2)}) %all-to-all-start) | async-done | bytes 393248 | tf_op jit(solution)/shard_map/all_to_all | solution.py:468
  29.2 0.0 copy-done
  29.2 0.0 copy-done.1
  29.2 5.6 %apply.1 = (bf16[128,384]{1,0:T(8,128)(2,1)}, bf16[64,768]{1,0:T(8,128)(2,1)}) custom-call(bf16[16,32,384]{2,1,0:T(8,128)(2,1)S(1)} %all-to-all-done.recv, bf16[25,1024,128]{2,1,0:T(8,128)(2,1)} %counts.1.table, bf16[192,3072]{1,0:T(8,128)(2,1)S(1)} %copy-done, bf16[192,3072]{1,0:T(8,128)(2,1)S(1)} %copy-done.1), custom_call_target="tpu_custom_call" | custom-call | flops 3000000000 | bytes 8000000 | tf_op jit(solution)/shard_map/apply/pallas_call | solution.py:419
Async XLA Ops:
  3.1 5.4 %collective-permute-start = (bf16[16,16,384]{2,1,0:T(8,128)(2,1)}, bf16[16,16,384]{2,1,0:T(8,128)(2,1)S(1)}, u32[]{:S(2)}, u32[]{:S(2)}) collective-permute-start(bf16[16,16,384]{2,1,0:T(8,128)(2,1)} %get-tuple-element.6), channel_id=1, source_target_pairs={{8,24},{9,25},{10,26},{11,27},{12,28},{13,29},{14,30},{15,31},{24,... | collective-permute-start | bytes 589832 | tf_op jit(solution)/shard_map/ppermute | solution.py:466
  9.2 20.0 %all-to-all-start = ((bf16[16,32,384]{2,1,0:T(8,128)(2,1)}), bf16[16,32,384]{2,1,0:T(8,128)(2,1)S(1)}, u32[]{:S(2)}, u32[]{:S(2)}) async-start(bf16[16,32,384]{2,1,0:T(8,128)(2,1)} %merge.1), calls=%async_computation | async-start | bytes 786432 | tf_op jit(solution)/shard_map/all_to_all | solution.py:468
  18.0 11.2 %copy-start = (bf16[192,3072]{1,0:T(8,128)(2,1)S(1)}, bf16[192,3072]{1,0:T(8,128)(2,1)}, u32[]{:S(2)}) copy-start(bf16[192,3072]{1,0:T(8,128)(2,1)} %fop.1) | copy-start | bytes 3538948
  18.1 11.2 %copy-start.1 = (bf16[192,3072]{1,0:T(8,128)(2,1)S(1)}, bf16[192,3072]{1,0:T(8,128)(2,1)}, u32[]{:S(2)}) copy-start(bf16[192,3072]{1,0:T(8,128)(2,1)} %cop.1) | copy-start | bytes 3538948

commit v4 on v3

--- a/solution.py
+++ b/solution.py
@@ -330,28 +330,23 @@
     def add_high(self, h_v, sem):
         boxes, planes = self.boxes, self.planes
 
-        flags = slice(self.flag_at, self.flag_at + self.slots)
-
-        @pl.when(jnp.max(self.flag_ref[...].astype(F32)[flags]) > 0.0)
-        def _():
-            for slot in range(self.slots):
-                for first in (slot * boxes, self.count + slot * boxes):
-                    self.split_ref[first : first + boxes, :] = jnp.zeros((boxes, 2 * self.depth), BF)
-
-                at = self.flag_at + slot
-
-                @pl.when(jnp.max(self.flag_ref[...].astype(F32)[at : at + 1, :]) > 0.0)
-                def _(slot=slot):
-                    first = self.n_ref.shape[0] + 1 + self.plane + slot * planes
-                    copy = pltpu.make_async_copy(self.table.at[pl.ds(first, planes)], h_v.at[pl.ds(0, planes)], sem)
-                    copy.start()
-                    copy.wait()
-                    sides = self.sources(slot)
-                    for g in range(8 // self.many):
-                        self.split(slot, sides, h_v, 0, g)
-
-            for odd in range(2):
-                self.total_ref[odd] = self.total_ref[odd] + 256.0 * self.operate(odd)
+        for slot in range(self.slots):
+            for first in (slot * boxes, self.count + slot * boxes):
+                self.split_ref[first : first + boxes, :] = jnp.zeros((boxes, 2 * self.depth), BF)
+            at = self.flag_at + slot
+
+            @pl.when(jnp.max(self.flag_ref[...].astype(F32)[at : at + 1, :]) > 0.0)
+            def _(slot=slot):
+                first = self.n_ref.shape[0] + 1 + self.plane + slot * planes
+                copy = pltpu.make_async_copy(self.table.at[pl.ds(first, planes)], h_v.at[pl.ds(0, planes)], sem)
+                copy.start()
+                copy.wait()
+                sides = self.sources(slot)
+                for g in range(8 // self.many):
+                    self.split(slot, sides, h_v, 0, g)
+
+        for odd in range(2):
+            self.total_ref[odd] = self.total_ref[odd] + 256.0 * self.operate(odd)
 
     def finish(self):
         boxes = self.boxes
@@ -372,11 +367,11 @@
 ):
     fine_slots, coarse_slots = fine_out.shape[1] // C, coarse_out.shape[1] // C
     last = 4 * fine_slots
+    flag_copy = fetch([(table.at[n_v.shape[0], 0:16, :], flag_v)], sems)[0]
     pieces = [slice(p, p + 2) for p in range(0, last, 2)]
-    fine_waits = fetch([(table.at[p], n_v.at[p]) for p in pieces], sems, 2)
-    tail = slice(last, last + coarse_slots)
-    rest = [(table.at[n_v.shape[0], 0:16, :], flag_v), (table.at[tail], n_v.at[tail])]
-    rest = fetch(rest, sems, 2 + len(pieces))
+    ahead = len(pieces)
+    pieces += [slice(last, last + coarse_slots)]
+    waits = fetch([(table.at[p], n_v.at[p]) for p in pieces], sems, 2)
 
     def fine_window(slot):
         at = (slot % 2) * 128
@@ -396,20 +391,25 @@
     ends = ((fine_o, fine_split, fine_total, 128), (coarse_o, coarse_split, coarse_total, 64))
     fine = Level(fine_window, n_v, 0, flag_v, 0, table, fop, *ends[0])
     coarse = Level(coarse_window, n_v, last, flag_v, fine_slots, table, cop, *ends[1])
-    fine.gather(fine_waits)
-    for copy in rest:
-        copy.wait()
+    flag_copy.wait()
+    some = jnp.max(flag_v[...].astype(F32)) > 0.0
+    fine.gather(waits[:ahead])
+    waits[ahead].wait()
     fine.translate()
     coarse.gather([])
     coarse.translate()
-    fine.add_high(h_v, sems.at[0])
-    coarse.add_high(h_v, sems.at[0])
+
+    @pl.when(some)
+    def _():
+        coarse.add_high(h_v, sems.at[0])
+        fine.add_high(h_v, sems.at[0])
+
     fine.finish()
-    done = pltpu.make_async_copy(fine_o, fine_out, sems.at[1])
-    done.start()
+    done = fetch([(fine_o, fine_out)], sems)
     coarse.finish()
-    pltpu.sync_copy(coarse_o, coarse_out)
-    done.wait()
+    done += fetch([(coarse_o, coarse_out)], sems, 1)
+    for copy in done:
+        copy.wait()
 
 
 def apply(recv, table, fine_operators, coarse_operators, fine_shape, coarse_shape):
@@ -431,7 +431,7 @@
             pltpu.VMEM((2, rows, 256), F32),
             pltpu.VMEM((2, rows, 256), F32),
             pltpu.VMEM((4, 1024, 128), BF),
-            pltpu.SemaphoreType.DMA((8,)),
+            pltpu.SemaphoreType.DMA((12,)),
         ],
         compiler_params=pltpu.CompilerParams(vmem_limit_bytes=LIMIT),
         cost_estimate=pl.CostEstimate(flops=3_000_000_000, bytes_accessed=8_000_000, transcendentals=0),

time: 35.2 us -> 35.1 us (level)
  the two profiles are of different devices: /device:TPU:96 before, /device:TPU:224 now
where the time goes in v4:
time: 35.1 us; the launch traced here: 34.8 us
  Pallas kernels  16.6 us (47%)
  starting transfers between devices  10.8 us (31%)
  waiting for transfers between devices  6.11 us (17%)
  between operations  0.69 us (2%)
  other arithmetic  0.64 us (2%)
    all_to_all x1, starting transfers between devices, per_device(): lax.all_to_all(packed, 'dir', split_axis=0, concat_axis=0, tiled=True)  8.84 us
    pallas_call x1, Pallas kernels, counts(): pl.pallas_call(count_kernel, out_shape=sds((2 * planes + 1, 1024, 128), B...  7.86 us
    pallas_call x1, Pallas kernels, apply(): pl.pallas_call(apply_kernel, out_shape=outs, in_specs=[VMEM, HBM, VMEM, V...  5.55 us
    all_to_all x1, waiting for transfers between devices, per_device(): lax.all_to_all(packed, 'dir', split_axis=0, concat_axis=0, tiled=True)  3.27 us
    ppermute x1, waiting for transfers between devices, per_device(): packed = merge(lax.ppermute(mine, ('box', 'dir'), route), packed)  2.83 us
    pallas_call x1, Pallas kernels, pack(): pl.pallas_call(pack_kernel, out_shape=(sds((peers, 16, 2 * C), BF), sds((...  2.42 us
    ppermute x1, starting transfers between devices, per_device(): packed = merge(lax.ppermute(mine, ('box', 'dir'), route), packed)  1.92 us
    pallas_call x1, Pallas kernels, merge(): pl.pallas_call(merge_kernel, out_shape=jax.ShapeDtypeStruct(packed.shape,...  0.73 us
  transfers between devices with their start and end apart: 2, of which 2 were waited for; matrix products, arithmetic and copies ran while one was open for 2% of the time, Pallas kernels for 23%

profile of v4, /device:TPU:224, one launch (start us, length us, event | category | flops | bytes accessed | tf_op | source)
XLA Modules:
  0.0 34.8 jit_solution(12473390012479993072)
XLA Ops:
  0.6 2.4 %pack.1 = (bf16[16,16,384]{2,1,0:T(8,128)(2,1)}, bf16[16,32,384]{2,1,0:T(8,128)(2,1)}) custom-call(s32[32]{0:T(128)} %fb.1, s32[64]{0:T(128)} %cb.1, bf16[8,6144]{1,0:T(8,128)(2,1)} %fd.1, bf16[4,12288]{1,0:T(4,128)(2,1)} %cd.1), custom_call_target="tpu_custom_call" | custom-call | flops 4000000 | bytes 800000 | tf_op jit(solution)/shard_map/pack/pallas_call | solution.py:89
  3.1 1.9 %collective-permute-start = (bf16[16,16,384]{2,1,0:T(8,128)(2,1)}, bf16[16,16,384]{2,1,0:T(8,128)(2,1)S(1)}, u32[]{:S(2)}, u32[]{:S(2)}) collective-permute-start(bf16[16,16,384]{2,1,0:T(8,128)(2,1)} %get-tuple-element.6), channel_id=1, source_target_pairs={{8,24},{9,25},{10,26},{11,27},{12,28},{13,29},{14,30},{15,31},{24,... | collective-permute-start | bytes 589832 | tf_op jit(solution)/shard_map/ppermute | solution.py:466
  5.0 0.6 %pad_add_fusion.firsts = s32[2]{0:T(128)} fusion(s32[1]{0:T(128)} %bitcast.1, s32[1]{0:T(128)} %bitcast), kind=kLoop, calls=%fused_computation | loop fusion | flops 2 | bytes 16 | tf_op jit(solution)/shard_map/stack | solution.py:462
  5.6 2.8 %collective-permute-done.near = bf16[16,16,384]{2,1,0:T(8,128)(2,1)S(1)} collective-permute-done((bf16[16,16,384]{2,1,0:T(8,128)(2,1)}, bf16[16,16,384]{2,1,0:T(8,128)(2,1)S(1)}, u32[]{:S(2)}, u32[]{:S(2)}) %collective-permute-start) | collective-permute-done | bytes 196640 | tf_op jit(solution)/shard_map/ppermute | solution.py:466
  8.5 0.7 %merge.1 = bf16[16,32,384]{2,1,0:T(8,128)(2,1)} custom-call(bf16[16,16,384]{2,1,0:T(8,128)(2,1)S(1)} %collective-permute-done.near, bf16[16,32,384]{2,1,0:T(8,128)(2,1)} %get-tuple-element.7._), custom_call_target="tpu_custom_call", output_to_operand_aliasing={{}: (1, {})} | custom-call | bytes 400000 | tf_op jit(solution)/shard_map/merge/pallas_call | solution.py:122
  9.2 8.8 %all-to-all-start = ((bf16[16,32,384]{2,1,0:T(8,128)(2,1)}), bf16[16,32,384]{2,1,0:T(8,128)(2,1)S(1)}, u32[]{:S(2)}, u32[]{:S(2)}) async-start(bf16[16,32,384]{2,1,0:T(8,128)(2,1)} %merge.1), calls=%async_computation | async-start | bytes 786432 | tf_op jit(solution)/shard_map/all_to_all | solution.py:468
  18.0 0.0 copy-start
  18.1 0.0 copy-start.1
  18.1 7.9 %counts.1.table = bf16[25,1024,128]{2,1,0:T(8,128)(2,1)} custom-call(s32[2]{0:T(128)} %pad_add_fusion.firsts, s32[2,2048]{1,0:T(2,128)} %fs.1, s32[2,2048]{1,0:T(2,128)} %ft.1, s32[2,2048]{1,0:T(2,128)} %fo.1, s32[4,1024]{1,0:T(4,128)} %cs.1, s32[4,1024]{1,0:T(4,128)} %ct.1, s32[4,1024]{1,0:T(4,128)} %co.1), custom_call_target="tpu_custom_call" | custom-call | flops 8999999488 | bytes 8000000 | tf_op jit(solution)/shard_map/counts/pallas_call | solution.py:245
  25.9 3.3 %all-to-all-done.recv = bf16[16,32,384]{2,1,0:T(8,128)(2,1)S(1)} async-done(((bf16[16,32,384]{2,1,0:T(8,128)(2,1)}), bf16[16,32,384]{2,1,0:T(8,128)(2,1)S(1)}, u32[]{:S(2)}, u32[]{:S(2)}) %all-to-all-start) | async-done | bytes 393248 | tf_op jit(solution)/shard_map/all_to_all | solution.py:468
  29.2 0.0 copy-done
  29.2 0.0 copy-done.1
  29.2 5.6 %apply.1 = (bf16[128,384]{1,0:T(8,128)(2,1)}, bf16[64,768]{1,0:T(8,128)(2,1)}) custom-call(bf16[16,32,384]{2,1,0:T(8,128)(2,1)S(1)} %all-to-all-done.recv, bf16[25,1024,128]{2,1,0:T(8,128)(2,1)} %counts.1.table, bf16[192,3072]{1,0:T(8,128)(2,1)S(1)} %copy-done, bf16[192,3072]{1,0:T(8,128)(2,1)S(1)} %copy-done.1), custom_call_target="tpu_custom_call" | custom-call | flops 3000000000 | bytes 8000000 | tf_op jit(solution)/shard_map/apply/pallas_call | solution.py:419
Async XLA Ops:
  3.1 5.4 %collective-permute-start = (bf16[16,16,384]{2,1,0:T(8,128)(2,1)}, bf16[16,16,384]{2,1,0:T(8,128)(2,1)S(1)}, u32[]{:S(2)}, u32[]{:S(2)}) collective-permute-start(bf16[16,16,384]{2,1,0:T(8,128)(2,1)} %get-tuple-element.6), channel_id=1, source_target_pairs={{8,24},{9,25},{10,26},{11,27},{12,28},{13,29},{14,30},{15,31},{24,... | collective-permute-start | bytes 589832 | tf_op jit(solution)/shard_map/ppermute | solution.py:466
  9.2 20.0 %all-to-all-start = ((bf16[16,32,384]{2,1,0:T(8,128)(2,1)}), bf16[16,32,384]{2,1,0:T(8,128)(2,1)S(1)}, u32[]{:S(2)}, u32[]{:S(2)}) async-start(bf16[16,32,384]{2,1,0:T(8,128)(2,1)} %merge.1), calls=%async_computation | async-start | bytes 786432 | tf_op jit(solution)/shard_map/all_to_all | solution.py:468
  18.0 11.2 %copy-start = (bf16[192,3072]{1,0:T(8,128)(2,1)S(1)}, bf16[192,3072]{1,0:T(8,128)(2,1)}, u32[]{:S(2)}) copy-start(bf16[192,3072]{1,0:T(8,128)(2,1)} %fop.1) | copy-start | bytes 3538948
  18.1 11.2 %copy-start.1 = (bf16[192,3072]{1,0:T(8,128)(2,1)S(1)}, bf16[192,3072]{1,0:T(8,128)(2,1)}, u32[]{:S(2)}) copy-start(bf16[192,3072]{1,0:T(8,128)(2,1)} %cop.1) | copy-start | bytes 3538948
